TPU v7x, 128 devices: a whole 4x4x4 slice. The times are simulated.
128 devices in a mesh: wide: 8 (over y, core), narrow: 16 (over z, x).
Axes of the slice: x: 4, y: 4, z: 4, core: 2. Of those that a mesh axis runs over, the one named last changes fastest.
Arguments:
- positions: float32 [3, 8, 16, 1, 128], P(None, 'wide', 'narrow'), may hold values from 0.08 to 0.92
- species: int32 [8, 16, 1, 128], P('wide', 'narrow'), may hold values 0 or 1
- neighbours: int32 [8, 16, 1, 128, 128], P('wide', 'narrow'), may hold values from 0 to 3455
- embed_one_w: float32 [2, 25], replicated, may hold values from -12 to 12
- embed_one_b: float32 [2, 25], replicated, may hold values from -6 to 6
- embed_two_w: float32 [25, 50], replicated, may hold values from -1.25 to 1.25
- embed_two_b: float32 [50], replicated, may hold values from -3 to 3
- embed_three_w: float32 [50, 100], replicated, may hold values from -0.875 to 0.875
- embed_three_b: float32 [100], replicated, may hold values from -3 to 3
- fit_one_w: float32 [1600, 240], replicated, may hold values from -0.15625 to 0.15625
- fit_one_b: float32 [240], replicated, may hold values from -6 to 6
- fit_two_w: float32 [240, 240], replicated, may hold values from -0.375 to 0.375
- fit_two_b: float32 [240], replicated, may hold values from -3 to 3
- fit_three_w: float32 [240, 240], replicated, may hold values from -0.375 to 0.375
- fit_three_b: float32 [240], replicated, may hold values from -3 to 3
- fit_out_w: float32 [240, 100], replicated, may hold values from -0.375 to 0.375
Outputs:
- dipole: float32 [3, 8, 16, 1, 128], P(None, 'wide', 'narrow')
- atom_field: float32 [4, 8, 16, 1, 128], P(None, 'wide', 'narrow')
- centroid_field: float32 [4, 8, 16, 1, 128], P(None, 'wide', 'narrow')
- energy: float32 [], replicated
Inputs may be any that keep to these rules, and one draw needn't show every extreme that they name: `species`: 1 marks a hydrogen, 0 an oxygen. `neighbours`: entry c names slot c % 128 of the brick offset by (q // 9 - 1, q % 3 - 1, (q // 3) % 3 - 1) bricks along x, y, z from the atom's own, q = c // 128, periodically; an entry may name the atom itself.
All inputs are finite; a program needn't handle non-finite values. No bound on the sum of `species` on one device may be relied on, other than what follows from the above.
Results may differ from a plain program's by a relative error of at most 0.0003.
Values sent between devices are 32-bit elements; how exact they have to be, the bound alone decides.
A program may use at most 64 MiB of HBM per device.

v0:
```python
import functools
import math

import jax
import jax.numpy as jnp
from jax import lax
from jax.sharding import Mesh
from jax.sharding import PartitionSpec as P

GRID_X = 256
GRID_Y = 256
GRID_Z = 256
AXIS_COLUMNS = 16
WIDE = ("wide_0", "wide_1")
NARROW = ("narrow_0", "narrow_1")
WIDE_NARROW = ("wide_0", "wide_1", "narrow_0", "narrow_1")


radius_scale = 24.0
wannier_reach = 0.5
ewald_beta = 0.9
coulomb = 0.25
atom_block = 64
largest_value = lax.Precision.HIGHEST


def extended(x, sides, width):
    for axis, dim in sides:
        size, length = (lax.axis_size(axis), x.shape[dim])
        up = [(i, (i + 1) % size) for i in range(size)]
        down = [(j, i) for i, j in up]
        last = lax.slice_in_dim(x, length - width, length, axis=dim)
        leading = lax.slice_in_dim(x, 0, width, axis=dim)
        before = lax.ppermute(last, axis, up)
        after = lax.ppermute(leading, axis, down)
        x = jnp.concatenate([before, x, after], axis=dim)
    return x


def shifted(x, axis, by):
    length = lax.axis_size(axis)
    return lax.ppermute(x, axis, [(i, (i + by) % length) for i in range(length)])


def over_axes(x, axes):
    return functools.reduce(lax.psum, axes, x)


def spline(offset):
    square = offset * offset
    offset_cube = square * offset
    remain = 4.0 - offset
    piece_one = offset_cube / 6.0
    piece_two = (-3.0 * offset_cube + 12.0 * square - 12.0 * offset + 4.0) / 6.0
    piece_three = (3.0 * offset_cube - 24.0 * square + 60.0 * offset - 44.0) / 6.0
    piece_four = remain * remain * remain / 6.0
    result_value = jnp.where(
        offset < 1.0,
        piece_one,
        jnp.where(offset < 2.0, piece_two, jnp.where(offset < 3.0, piece_three, piece_four)),
    )
    inside = (offset >= 0.0) & (offset < 4.0)
    return jnp.where(inside, result_value, jnp.zeros_like(offset))


def slope(offset):
    square = offset * offset
    remain = 4.0 - offset
    piece_one = square / 2.0
    piece_two = (-9.0 * square + 24.0 * offset - 12.0) / 6.0
    piece_three = (9.0 * square - 48.0 * offset + 60.0) / 6.0
    piece_four = -remain * remain / 2.0
    result_value = jnp.where(
        offset < 1.0,
        piece_one,
        jnp.where(offset < 2.0, piece_two, jnp.where(offset < 3.0, piece_three, piece_four)),
    )
    inside = (offset >= 0.0) & (offset < 4.0)
    return jnp.where(inside, result_value, jnp.zeros_like(offset))


def environment(
    relative, hydrogen, one_w, one_b, second_weight, second_bias, third_weight, third_bias
):
    scaled = relative / radius_scale
    square = jnp.sum(scaled * scaled, axis=0)
    smooth = 1.0 / (1.0 + square)
    radial = jnp.concatenate([smooth[None], smooth[None] * scaled], axis=0)
    is_hydrogen = hydrogen[None] > 0.5
    weight = jnp.where(is_hydrogen, one_w[1][:, None, None], one_w[0][:, None, None])
    offset_b = jnp.where(is_hydrogen, one_b[1][:, None, None], one_b[0][:, None, None])
    first_layer = jnp.tanh(weight * smooth[None] + offset_b)
    second_layer = jnp.tanh(
        jnp.einsum("tky,ti->iky", first_layer, second_weight, precision=largest_value)
        + second_bias[:, None, None]
    ) + jnp.concatenate([first_layer, first_layer], axis=0)
    third_layer = jnp.tanh(
        jnp.einsum("tky,ti->iky", second_layer, third_weight, precision=largest_value)
        + third_bias[:, None, None]
    ) + jnp.concatenate([second_layer, second_layer], axis=0)
    return (
        jnp.einsum("pbn,dbn->pdb", radial, third_layer, precision=largest_value) / relative.shape[2]
    )


def fitting(matrix, one_w, one_b, second_weight, second_bias, third_weight, third_bias, out_w):
    descriptor = jnp.einsum(
        "pda,pea->dea", matrix, matrix[:, :AXIS_COLUMNS], precision=largest_value
    )
    descriptor = descriptor.reshape(-1, matrix.shape[2])
    hidden = jnp.tanh(
        jnp.einsum("fh,fa->ha", one_w, descriptor, precision=largest_value) + one_b[:, None]
    )
    hidden = hidden + jnp.tanh(
        jnp.einsum("gh,ga->ha", second_weight, hidden, precision=largest_value)
        + second_bias[:, None]
    )
    hidden = hidden + jnp.tanh(
        jnp.einsum("gh,ga->ha", third_weight, hidden, precision=largest_value) + third_bias[:, None]
    )
    coeffs = jnp.einsum("hk,ha->ka", out_w, hidden, precision=largest_value)
    return jnp.einsum("ka,cka->ca", coeffs, matrix[1:], precision=largest_value)


def folded(mode_index, length):
    wrapped = mode_index % length
    return jnp.where(2 * wrapped >= length, wrapped - length, wrapped)


def modulus(mode_index, length):
    phase_angle = (mode_index % length).astype(jnp.float32) * (2.0 * math.pi / length)
    divisor = (4.0 + 2.0 * jnp.cos(phase_angle)) / 6.0
    return 1.0 / (divisor * divisor)


def influence(index_x, index_y, index_z):
    fold_x = folded(index_x, GRID_X)
    fold_y = folded(index_y, GRID_Y)
    fold_z = folded(index_z, GRID_Z)
    freq_x = fold_x.astype(jnp.float32) / GRID_X
    freq_y = fold_y.astype(jnp.float32) / GRID_Y
    freq_z = fold_z.astype(jnp.float32) / GRID_Z
    square = freq_x * freq_x + freq_y * freq_y + freq_z * freq_z
    is_zero = (fold_x == 0) & (fold_y == 0) & (fold_z == 0)
    safe_square = jnp.where(is_zero, 1.0, square)
    result_value = jnp.exp(-(math.pi * math.pi) * square / (ewald_beta * ewald_beta)) / safe_square
    result_value = (
        result_value
        * modulus(index_x, GRID_X)
        * modulus(index_y, GRID_Y)
        * modulus(index_z, GRID_Z)
    )
    return jnp.where(is_zero, 0.0, result_value) * (coulomb / (math.pi * GRID_X * GRID_Y * GRID_Z))


def phases(length):
    counter = jnp.arange(length, dtype=jnp.int32)
    product = counter[:, None] * counter[None, :] % length
    phase_angle = product.astype(jnp.float32) * (2.0 * math.pi / length)
    return (jnp.cos(phase_angle), jnp.sin(phase_angle))


def rotate(real_part, imag_part, cos_table, sin_table, pattern, direction):
    real_cos = jnp.einsum(pattern, real_part, cos_table, precision=largest_value)
    real_sin = jnp.einsum(pattern, real_part, sin_table, precision=largest_value)
    imag_cos = jnp.einsum(pattern, imag_part, cos_table, precision=largest_value)
    imag_sin = jnp.einsum(pattern, imag_part, sin_table, precision=largest_value)
    return (real_cos - direction * imag_sin, imag_cos + direction * real_sin)


def spline_rows(coordinate, lowest, cell_count):
    grid_cells = jnp.arange(cell_count, dtype=jnp.int32).astype(jnp.float32) + lowest
    offset = coordinate[None, :] - grid_cells[:, None]
    return (spline(offset), slope(offset))


def mirrored(plane):
    return jnp.roll(jnp.flip(plane, (0, 1)), 1, (0, 1))


def local(
    positions,
    species,
    neighbours,
    embed_one_w,
    embed_one_b,
    embed_two_w,
    embed_two_b,
    embed_three_w,
    embed_three_b,
    fit_one_w,
    fit_one_b,
    fit_two_w,
    fit_two_b,
    fit_three_w,
    fit_three_b,
    fit_out_w,
):
    wide_count = lax.axis_size(WIDE)
    narrow_count = lax.axis_size(NARROW)
    pieces = wide_count * narrow_count
    bricks = positions.shape[3]
    per_brick = positions.shape[4]
    atom_count = bricks * per_brick
    listed = neighbours.shape[4]
    cells_x = GRID_X // wide_count
    cells_z = GRID_Z // narrow_count
    brick_y = GRID_Y // bricks
    hydrogen = species.reshape(atom_count).astype(jnp.float32)
    packed = jnp.concatenate([positions, species.astype(jnp.float32)[None]], axis=0)
    ghosts = extended(packed, ((WIDE, 1), (NARROW, 2)), 1)
    own_atoms = positions.reshape(3, atom_count)
    code_table = neighbours.reshape(atom_count, listed)
    slot_index = code_table % per_brick
    offset = code_table // per_brick
    step_x = offset // 9
    step_z = offset // 3 % 3
    step_y = offset % 3
    home_brick = (jnp.arange(atom_count, dtype=jnp.int32) // per_brick)[:, None]
    source = (
        (step_x * 3 + step_z) * bricks + (home_brick + step_y - 1) % bricks
    ) * per_brick + slot_index
    ghost_table = ghosts.reshape(4, 9 * atom_count)
    nearby = jnp.take(ghost_table, source, axis=1)
    extent = jnp.array([cells_x, brick_y, cells_z], jnp.float32)[:, None, None]
    steps_all = jnp.stack([step_x, step_y, step_z]) - 1
    relative = (
        steps_all.astype(jnp.float32) * extent + (nearby[:3] - own_atoms[:, :, None]) * extent
    )
    block_size = min(atom_block, atom_count)
    block_count = atom_count // block_size
    rel_blocks = relative.reshape(3, block_count, block_size, listed).transpose(1, 0, 2, 3)
    kind_blocks = nearby[3].reshape(block_count, block_size, listed)

    def one_block(operands):
        return environment(
            operands[0],
            operands[1],
            embed_one_w,
            embed_one_b,
            embed_two_w,
            embed_two_b,
            embed_three_w,
            embed_three_b,
        )

    matrix = lax.map(one_block, (rel_blocks, kind_blocks))
    matrix = matrix.transpose(1, 2, 0, 3).reshape(4, matrix.shape[2], atom_count)
    dipole = fitting(
        matrix, fit_one_w, fit_one_b, fit_two_w, fit_two_b, fit_three_w, fit_three_b, fit_out_w
    )
    oxygen = 1.0 - hydrogen
    home_y = (jnp.arange(atom_count, dtype=jnp.int32) // per_brick).astype(jnp.float32)
    atom_x = own_atoms[0] * cells_x
    atom_y = home_y * brick_y + own_atoms[1] * brick_y
    atom_z = own_atoms[2] * cells_z
    displace = wannier_reach * jnp.tanh(dipole)
    site_x = jnp.concatenate([atom_x, atom_x + displace[0]])
    site_y = jnp.concatenate([atom_y, atom_y + displace[1]])
    site_z = jnp.concatenate([atom_z, atom_z + displace[2]])
    charge = jnp.concatenate([6.0 * oxygen + hydrogen, -8.0 * oxygen])
    site_count = 2 * atom_count
    weight_x, slope_x = spline_rows(site_x, -3.0, cells_x + 3)
    weight_z, slope_z = spline_rows(site_z, -3.0, cells_z + 3)
    cells_y = jnp.arange(GRID_Y, dtype=jnp.int32).astype(jnp.float32)
    offset_y = jnp.mod(site_y[None, :] - cells_y[:, None], float(GRID_Y))
    weight_y = spline(offset_y)
    slope_y = slope(offset_y)
    mixed_rows = (weight_z[:, None, :] * weight_x[None, :, :] * charge[None, None, :]).reshape(
        -1, site_count
    )
    spread = lax.dot_general(
        mixed_rows, weight_y, (((1,), (1,)), ((), ())), precision=largest_value
    )
    spread = spread.reshape(cells_z + 3, cells_x + 3, GRID_Y)
    rim_x = shifted(spread[:, :3], WIDE, -1)
    inner_rows = spread[:, 3:]
    inner_rows = jnp.concatenate(
        [inner_rows[:, : cells_x - 3], inner_rows[:, cells_x - 3 :] + rim_x], axis=1
    )
    rim_z = shifted(inner_rows[:3], NARROW, -1)
    inner_rows = inner_rows[3:]
    charge_grid = jnp.concatenate(
        [inner_rows[: cells_z - 3], inner_rows[cells_z - 3 :] + rim_z], axis=0
    )
    cos_y, sin_y = phases(GRID_Y)
    mode_count = GRID_Y // 2
    counter = jnp.arange(GRID_Y, dtype=jnp.int32)
    alternate = (1 - 2 * (counter % 2)).astype(jnp.float32)
    first_mode = jnp.arange(mode_count, dtype=jnp.int32) == 0
    cos_fwd = cos_y[:, :mode_count]
    sin_fwd = jnp.where(first_mode[None, :], -alternate[:, None], sin_y[:, :mode_count])
    doubled = jnp.where(first_mode, 1.0, 2.0)[:, None]
    cos_back = cos_y[:mode_count] * doubled
    sin_back = jnp.where(first_mode[:, None], -alternate[None, :], 2.0 * sin_y[:mode_count])
    fine_modes = mode_count // pieces
    cos_x, sin_x = phases(GRID_X)
    cos_z, sin_z = phases(GRID_Z)
    table_xc = cos_x.reshape(wide_count, cells_x, GRID_X)
    table_xs = sin_x.reshape(wide_count, cells_x, GRID_X)
    table_zc = cos_z.reshape(narrow_count, cells_z, GRID_Z)
    table_zs = sin_z.reshape(narrow_count, cells_z, GRID_Z)
    real_part = jnp.einsum(
        "zxy,ypj->pzxj",
        charge_grid,
        cos_fwd.reshape(GRID_Y, pieces, fine_modes),
        precision=largest_value,
    )
    imag_part = -jnp.einsum(
        "zxy,ypj->pzxj",
        charge_grid,
        sin_fwd.reshape(GRID_Y, pieces, fine_modes),
        precision=largest_value,
    )
    outgoing = jnp.stack([real_part, imag_part]).reshape(2, pieces, cells_z * cells_x * fine_modes)
    arrived = lax.all_to_all(outgoing, WIDE_NARROW, split_axis=1, concat_axis=1, tiled=True)
    arrived = arrived.reshape(2, wide_count, narrow_count, cells_z, cells_x, fine_modes)
    real_part, imag_part = rotate(
        arrived[0], arrived[1], table_xc, table_xs, "wnzxj,wxm->nzjm", -1.0
    )
    real_part, imag_part = rotate(real_part, imag_part, table_zc, table_zs, "nzjm,nzk->jmk", -1.0)
    piece_index = lax.axis_index(WIDE) * narrow_count + lax.axis_index(NARROW)
    index_y = (piece_index * fine_modes + jnp.arange(fine_modes, dtype=jnp.int32))[:, None, None]
    index_x = jnp.arange(GRID_X, dtype=jnp.int32)[None, :, None]
    index_z = jnp.arange(GRID_Z, dtype=jnp.int32)[None, None, :]
    green_table = influence(index_x, index_y, index_z)
    is_first = piece_index == 0
    first_real = real_part[0]
    first_imag = imag_part[0]
    mirror_real = mirrored(first_real)
    mirror_imag = mirrored(first_imag)
    zero_real = 0.5 * (first_real + mirror_real)
    zero_imag = 0.5 * (first_imag - mirror_imag)
    top_real = 0.5 * (first_imag + mirror_imag)
    top_imag = 0.5 * (mirror_real - first_real)
    green_zero = green_table[0]
    green_top = influence(index_x[0], jnp.full((1, 1), GRID_Y // 2, jnp.int32), index_z[0])
    ordinary = green_table * (real_part * real_part + imag_part * imag_part)
    special = 0.5 * (
        green_zero * (zero_real * zero_real + zero_imag * zero_imag)
        + green_top * (top_real * top_real + top_imag * top_imag)
    )
    first_terms = jnp.where(is_first, special, ordinary[0])
    partial_modes = jnp.sum(ordinary[1:]) + jnp.sum(first_terms)
    packed_real = green_zero * zero_real - green_top * top_imag
    packed_imag = green_zero * zero_imag + green_top * top_real
    row_real = jnp.where(is_first, packed_real, green_zero * first_real)
    row_imag = jnp.where(is_first, packed_imag, green_zero * first_imag)
    real_part = jnp.concatenate([row_real[None], real_part[1:] * green_table[1:]], axis=0)
    imag_part = jnp.concatenate([row_imag[None], imag_part[1:] * green_table[1:]], axis=0)
    energy = over_axes(partial_modes, WIDE_NARROW) / (atom_count * pieces)
    real_part, imag_part = rotate(real_part, imag_part, table_zc, table_zs, "jmk,nzk->nzjm", 1.0)
    real_part, imag_part = rotate(real_part, imag_part, table_xc, table_xs, "nzjm,wxm->wnzxj", 1.0)
    outgoing = jnp.stack([real_part, imag_part]).reshape(2, pieces, cells_z * cells_x * fine_modes)
    arrived = lax.all_to_all(outgoing, WIDE_NARROW, split_axis=1, concat_axis=1, tiled=True)
    arrived = arrived.reshape(2, pieces, cells_z, cells_x, fine_modes)
    potential_grid = jnp.einsum(
        "pzxj,pjy->zxy",
        arrived[0],
        cos_back.reshape(pieces, fine_modes, GRID_Y),
        precision=largest_value,
    ) - jnp.einsum(
        "pzxj,pjy->zxy",
        arrived[1],
        sin_back.reshape(pieces, fine_modes, GRID_Y),
        precision=largest_value,
    )
    lower_z = shifted(potential_grid[cells_z - 3 :], NARROW, 1)
    grid_z = jnp.concatenate([lower_z, potential_grid], axis=0)
    lower_x = shifted(grid_z[:, cells_x - 3 :], WIDE, 1)
    grid_ext = jnp.concatenate([lower_x, grid_z], axis=1)
    flat_rows = grid_ext.reshape(-1, GRID_Y)
    value_rows = jnp.dot(flat_rows, weight_y, precision=largest_value).reshape(
        cells_z + 3, cells_x + 3, site_count
    )
    slope_rows = jnp.dot(flat_rows, slope_y, precision=largest_value).reshape(
        cells_z + 3, cells_x + 3, site_count
    )
    potential = jnp.einsum("zxs,zs,xs->s", value_rows, weight_z, weight_x, precision=largest_value)
    field_x = -jnp.einsum("zxs,zs,xs->s", value_rows, weight_z, slope_x, precision=largest_value)
    field_y = -jnp.einsum("zxs,zs,xs->s", slope_rows, weight_z, weight_x, precision=largest_value)
    field_z = -jnp.einsum("zxs,zs,xs->s", value_rows, slope_z, weight_x, precision=largest_value)
    fields = jnp.stack([potential, field_x, field_y, field_z])
    atom_field = fields[:, :atom_count].reshape(4, 1, 1, bricks, per_brick)
    centroid_field = (fields[:, atom_count:] * oxygen[None]).reshape(4, 1, 1, bricks, per_brick)
    dipole_out = (dipole * oxygen[None]).reshape(3, 1, 1, bricks, per_brick)
    return (dipole_out, atom_field, centroid_field, energy)


def solution(mesh):
    split = Mesh(mesh.devices.reshape(4, 2, 4, 4), ("wide_0", "wide_1", "narrow_0", "narrow_1"))
    placed = (
        P(None, WIDE, NARROW, None, None),
        P(WIDE, NARROW, None, None),
        P(WIDE, NARROW, None, None, None),
        P(),
        P(),
        P(),
        P(),
        P(),
        P(),
        P(),
        P(),
        P(),
        P(),
        P(),
        P(),
        P(),
    )
    return jax.shard_map(
        local,
        mesh=split,
        in_specs=placed,
        out_specs=(
            P(None, WIDE, NARROW, None, None),
            P(None, WIDE, NARROW, None, None),
            P(None, WIDE, NARROW, None, None),
            P(),
        ),
        check_vma=False,
    )
```

profile of v0, /device:TPU:34, one launch (start us, length us, event | category | flops | bytes accessed | tf_op | source)
XLA Modules:
  0.0 272.7 jit_solution(15856588607040213293)
XLA Ops:
  0.6 0.8 convert_bitcast_fusion
  2.1 3.0 %collective-permute-start.1 = (f32[4,1,1,1,128]{4,3,2,1,0:T(1,128)S(1)}, f32[4,1,1,1,128]{4,3,2,1,0:T(1,128)S(1)}, u32[]{:S(2)}, u32[]{:S(2)}) collective-permute-start(f32[4,1,1,1,128]{4,3,2,1,0:T(1,128)S(1)} %pad_maximum_fusion.12), channel_id=1, source_target_pairs={{16,0},{32,16},{48,32},{64,48},{80,64},{96,80},{112,96},{0,112},{1... | collective-permute-start | bytes 6152 | tf_op jit(solution)/shard_map/ppermute | solution.py:35
  5.1 1.0 fusion.255
  6.1 1.1 compare_and_fusion
  7.2 1.0 add_select_fusion.10
  8.2 1.2 bitcast_add_fusion.3
  10.6 1.7 fusion.197
  12.3 1.7 fusion.196
  15.9 1.5 collective-permute-start.2
  19.5 1.7 collective-permute-done.3
  22.2 54.8 %gather_fusion = f32[16384,4]{1,0:T(8,128)} fusion(f32[4,1152]{0,1:T(8,128)S(1)} %bitcast.356, s32[16384]{0:T(1024)S(1)} %fusion.255), kind=kCustom, calls=%fused_computation | custom fusion | bytes 589824 | tf_op jit(solution)/shard_map/jit(_take)/gather | solution.py:224
  77.0 5.3 %copy.39 = f32[128,128,4]{1,0,2:T(8,128)S(1)} copy(f32[128,128,4]{2,1,0:T(8,128)} %bitcast.358) | data formatting | bytes 524288 | tf_op jit(solution)/shard_map/jit(_take)/gather | solution.py:224
  82.7 22.7 %while.10 = (s32[]{:T(128)}, f32[2,4,100,64]{2,1,3,0:T(4,128)S(1)}, f32[2,64,128]{2,1,0:T(8,128)S(1)}, f32[2,25]{1,0:T(2,128)S(1)}, f32[2,3,64,128]{3,1,2,0:T(4,...) while((s32[]{:T(128)}, f32[2,4,100,64]{2,1,3,0:T(4,128)S(1)}, ...), condition=%wide.region_2.3_spmd, body=%wide.region_0.2_spmd.sunk | while | flops 658408448 | bytes 14297501 | solution.py:247
  83.2 1.9 maximum_add_fusion.12
  85.1 2.9 %fusion.495 = f32[64,128,100]{1,2,0:T(8,128)S(1)} fusion(f32[50,64,128]{2,0,1:T(8,128)S(1)} %maximum_add_fusion.12, f32[50,100]{1,0:T(8,128)S(1)} %get-tuple-element.232), kind=kOutput, calls=%fused_computation.24.clone.1 | convolution fusion | flops 491520000 | bytes 4935200 | tf_op jit(solution)/shard_map/while/body/eval_jaxpr/tky,ti->iky/dot_general | solution.py:98
  88.1 5.8 %fusion.496 = f32[2,4,100,64]{2,1,3,0:T(4,128)S(1)} fusion(f32[2,4,100,64]{2,1,3,0:T(4,128)S(1)} %get-tuple-element.214, s32[]{:T(128)} %get-tuple-element.213, f32[50,64,128]{2,0,1:T(8,128)S(1)} %maximum_add_fusion.12, f32[64,128,100]{1,2,0:T(8,128)S(1)} %fusion.495, f32[100]{0:T(128)S(1)} %get-tuple-element.233, ...), kind=kOutput, calls=%fused_computation.12.clone.1 | convolution fusion | flops 41837568 | bytes 5538308 | tf_op jit(solution)/shard_map/while/body/eval_jaxpr/pbn,dbn->pdb/dot_general | solution.py:102
  94.3 1.9 maximum_add_fusion.12
  96.2 2.9 %fusion.495 = f32[64,128,100]{1,2,0:T(8,128)S(1)} fusion(f32[50,64,128]{2,0,1:T(8,128)S(1)} %maximum_add_fusion.12, f32[50,100]{1,0:T(8,128)S(1)} %get-tuple-element.232), kind=kOutput, calls=%fused_computation.24.clone.1 | convolution fusion | flops 491520000 | bytes 4935200 | tf_op jit(solution)/shard_map/while/body/eval_jaxpr/tky,ti->iky/dot_general | solution.py:98
  99.2 5.8 %fusion.496 = f32[2,4,100,64]{2,1,3,0:T(4,128)S(1)} fusion(f32[2,4,100,64]{2,1,3,0:T(4,128)S(1)} %get-tuple-element.214, s32[]{:T(128)} %get-tuple-element.213, f32[50,64,128]{2,0,1:T(8,128)S(1)} %maximum_add_fusion.12, f32[64,128,100]{1,2,0:T(8,128)S(1)} %fusion.495, f32[100]{0:T(128)S(1)} %get-tuple-element.233, ...), kind=kOutput, calls=%fused_computation.12.clone.1 | convolution fusion | flops 41837568 | bytes 5538308 | tf_op jit(solution)/shard_map/while/body/eval_jaxpr/pbn,dbn->pdb/dot_general | solution.py:102
  106.1 2.9 %convolution_bitcast_fusion = f32[100,16,128]{0,1,2:T(8,128)S(1)} fusion(f32[4,100,128]{1,0,2:T(4,128)} %bitcast.361), kind=kOutput, calls=%fused_computation.33 | convolution fusion | flops 9830400 | bytes 1343488 | tf_op jit(solution)/shard_map/pda,pea->dea/dot_general | solution.py:107
  109.7 1.1 slice.199
  110.9 1.5 fusion.38
  115.3 1.2 fusion.39
  116.7 1.9 collective-permute-done.4
  118.7 1.0 collective-permute-start.5
  119.8 4.2 %collective-permute-done.5 = f32[3,32,256]{2,1,0:T(8,128)S(1)} collective-permute-done((f32[3,32,256]{2,1,0:T(8,128)S(1)}, f32[3,32,256]{2,1,0:T(8,128)S(1)}, u32[]{:S(2)}, u32[]{:S(2)}) %collective-permute-start.5) | collective-permute-done | bytes 98336 | tf_op jit(solution)/shard_map/ppermute | solution.py:42
  125.6 1.3 pad_maximum_fusion.1
  126.9 14.1 %all-to-all-start = ((f32[2,128,512]{2,0,1:T(2,128)}), f32[2,128,512]{2,0,1:T(2,128)S(1)}, u32[]{:S(2)}, u32[]{:S(2)}) async-start(f32[2,128,512]{2,0,1:T(2,128)} %pad_maximum_fusion.1), calls=%async_computation | async-start | bytes 1048576 | tf_op jit(solution)/shard_map/all_to_all | solution.py:316
  141.2 12.1 %all-to-all-done = f32[2,128,512]{2,0,1:T(2,128)S(1)} async-done(((f32[2,128,512]{2,0,1:T(2,128)}), f32[2,128,512]{2,0,1:T(2,128)S(1)}, u32[]{:S(2)}, u32[]{:S(2)}) %all-to-all-start) | async-done | bytes 524320 | tf_op jit(solution)/shard_map/all_to_all | solution.py:316
  153.3 1.4 slice_reduce_fusion.1
  155.0 1.3 reshape.1387
  156.3 1.9 convolution_bitcast_fusion.8
  158.2 3.1 %convolution_bitcast_fusion.10 = f32[16,16,256]{2,1,0:T(8,128)S(1)} fusion(f32[8,16,16,32]{3,2,1,0:T(8,128)} %reshape.1387, s32[8,32]{1,0:T(8,128)S(1)} %multiply_add_fusion.1), kind=kOutput, calls=%fused_computation.63 | convolution fusion | flops 202244096 | bytes 525312 | tf_op jit(solution)/shard_map/wnzxj,wxm->nzjm/dot_general | solution.py:164
  161.3 1.9 fusion.31
  163.3 1.9 fusion.33
  165.2 1.5 convolution_bitcast_fusion.4
  166.7 1.7 fusion.27
  168.5 1.5 convolution_bitcast_fusion.6
  170.0 1.5 fusion.29
  174.2 1.8 fusion.112
  176.0 1.8 fusion.108
  177.8 1.8 fusion.25
  179.6 2.0 fusion.106
  181.6 2.0 fusion.24
  183.6 3.0 %fusion.104 = f32[8,32,16,16]{1,3,2,0:T(8,128)} fusion(f32[16,16,256,1]{2,1,0,3:T(8,128)S(1)} %fusion.24, s32[8,32]{1,0:T(8,128)S(1)} %multiply_add_fusion.1), kind=kOutput, calls=%fused_computation.177 | convolution fusion | flops 202244096 | bytes 525312 | tf_op jit(solution)/shard_map/nzjm,wxm->wnzxj/dot_general | solution.py:166
  186.6 2.0 fusion.21
  188.6 1.2 stack.50
  189.8 3.3 %fusion.20 = f32[8,16,16,32,1]{3,2,1,0,4:T(8,128)S(1)} fusion(f32[8,32,16,16]{1,3,2,0:T(8,128)} %fusion.104, f32[16,16,256,1]{2,1,0,3:T(8,128)} %copy-done.13, s32[8,32]{1,0:T(8,128)S(1)} %multiply_add_fusion.1), kind=kOutput, calls=%fused_computation.35 | convolution fusion | flops 202309632 | bytes 787456 | tf_op jit(solution)/shard_map/nzjm,wxm->wnzxj/dot_general | solution.py:165
  193.1 1.2 stack.51
  194.3 2.3 pad_maximum_fusion.2
  196.6 5.7 %all-to-all-start.1 = ((f32[2,128,512]{2,0,1:T(2,128)}), f32[2,128,512]{2,0,1:T(2,128)S(1)}, u32[]{:S(2)}, u32[]{:S(2)}) async-start(f32[2,128,512]{2,0,1:T(2,128)} %pad_maximum_fusion.2), calls=%async_computation.1 | async-start | bytes 1048576 | tf_op jit(solution)/shard_map/all_to_all | solution.py:355
  202.8 12.0 %all-to-all-done.1 = f32[2,128,512]{2,0,1:T(2,128)S(1)} async-done(((f32[2,128,512]{2,0,1:T(2,128)}), f32[2,128,512]{2,0,1:T(2,128)S(1)}, u32[]{:S(2)}, u32[]{:S(2)}) %all-to-all-start.1) | async-done | bytes 524320 | tf_op jit(solution)/shard_map/all_to_all | solution.py:355
  214.8 1.1 fusion.452
  216.0 1.8 copy.47
  217.9 1.5 fusion.156
  219.4 1.7 convolution_subtract_fusion.1
  221.2 4.6 %collective-permute-done.6 = f32[3,32,256]{2,1,0:T(8,128)S(1)} collective-permute-done((f32[3,32,256]{2,1,0:T(8,128)S(1)}, f32[3,32,256]{2,1,0:T(8,128)S(1)}, u32[]{:S(2)}, u32[]{:S(2)}) %collective-permute-start.6) | collective-permute-done | bytes 98336 | tf_op jit(solution)/shard_map/ppermute | solution.py:42
  227.1 1.3 select_reduce_fusion
  228.4 9.4 %psum.28 = f32[]{:T(128)} all-reduce(f32[]{:T(128)} %select_reduce_fusion), channel_id=1, replica_groups=mesh['wide_0'=4,'wide_1'=2,'narrow_0'=4,'narrow_1'=4] {'wide_0'}, use_global_device_ids=true, to_apply=%region_4.5 | all-reduce | flops 1 | bytes 8 | tf_op jit(solution)/shard_map/psum | solution.py:46
  237.9 3.1 %psum.29 = f32[]{:T(128)} all-reduce(f32[]{:T(128)} %psum.28), channel_id=1, replica_groups=mesh['wide_0'=4,'wide_1'=2,'narrow_0'=4,'narrow_1'=4] {'wide_1'}, use_global_device_ids=true, to_apply=%region_5.6 | all-reduce | flops 1 | bytes 8 | tf_op jit(solution)/shard_map/psum | solution.py:46
  241.2 9.6 %psum.30 = f32[]{:T(128)} all-reduce(f32[]{:T(128)} %psum.29), channel_id=1, replica_groups=mesh['wide_0'=4,'wide_1'=2,'narrow_0'=4,'narrow_1'=4] {'narrow_0'}, use_global_device_ids=true, to_apply=%region_6.7 | all-reduce | flops 1 | bytes 8 | tf_op jit(solution)/shard_map/psum | solution.py:46
  251.3 13.3 %psum.31 = f32[]{:T(128)} all-reduce(f32[]{:T(128)} %psum.30), channel_id=1, replica_groups=mesh['wide_0'=4,'wide_1'=2,'narrow_0'=4,'narrow_1'=4] {'narrow_1'}, use_global_device_ids=true, to_apply=%region_7.8 | all-reduce | flops 1 | bytes 8 | tf_op jit(solution)/shard_map/psum | solution.py:46
  265.3 2.2 fusion.23
  267.7 2.2 multiply_reduce_fusion
  (187 shorter events, 21.1 us)
Async XLA Ops:
  0.6 110.2 %copy-start = (f32[1600,240]{0,1:T(8,128)S(1)}, f32[1600,240]{0,1:T(8,128)}, u32[]{:S(2)}) copy-start(f32[1600,240]{0,1:T(8,128)} %param.28) | copy-start | bytes 4608004
  2.1 13.1 %collective-permute-start = (f32[4,1,1,1,128]{4,3,2,1,0:T(1,128)S(1)}, f32[4,1,1,1,128]{4,3,2,1,0:T(1,128)S(1)}, u32[]{:S(2)}, u32[]{:S(2)}) collective-permute-start(f32[4,1,1,1,128]{4,3,2,1,0:T(1,128)S(1)} %pad_maximum_fusion.12), channel_id=1, source_target_pairs={{0,16},{16,32},{32,48},{48,64},{64,80},{80,96},{96,112},{112,0},{1... | collective-permute-start | bytes 6152 | tf_op jit(solution)/shard_map/ppermute | solution.py:34
  2.1 13.1 %collective-permute-start.1 = (f32[4,1,1,1,128]{4,3,2,1,0:T(1,128)S(1)}, f32[4,1,1,1,128]{4,3,2,1,0:T(1,128)S(1)}, u32[]{:S(2)}, u32[]{:S(2)}) collective-permute-start(f32[4,1,1,1,128]{4,3,2,1,0:T(1,128)S(1)} %pad_maximum_fusion.12), channel_id=1, source_target_pairs={{16,0},{32,16},{48,32},{64,48},{80,64},{96,80},{112,96},{0,112},{1... | collective-permute-start | bytes 6152 | tf_op jit(solution)/shard_map/ppermute | solution.py:35
  9.4 104.9 %copy-start.24 = (f32[128]{0:T(128)}, f32[128]{0:T(128)S(1)}, u32[]{:S(2)}) copy-start(f32[128]{0:T(128)S(1)} %get-tuple-element.118) | copy-start | bytes 1540
  14.0 110.8 %copy-start.28 = (f32[256]{0:T(256)}, f32[256]{0:T(256)S(1)}, u32[]{:S(2)}) copy-start(f32[256]{0:T(256)S(1)} %fusion.340) | copy-start | bytes 3076
  15.9 3.6 %collective-permute-start.2 = (f32[4,3,1,1,128]{4,3,2,1,0:T(1,128)S(1)}, f32[4,3,1,1,128]{4,3,2,1,0:T(1,128)S(1)}, u32[]{:S(2)}, u32[]{:S(2)}) collective-permute-start(f32[4,3,1,1,128]{4,3,2,1,0:T(1,128)S(1)} %pad_maximum_fusion.10), channel_id=1, source_target_pairs={{0,1},{1,2},{2,3},{3,4},{4,5},{5,6},{6,7},{7,8},{8,9},{9,10},{10,1... | collective-permute-start | bytes 18440 | tf_op jit(solution)/shard_map/ppermute | solution.py:34
  17.4 3.8 %collective-permute-start.3 = (f32[4,3,1,1,128]{4,3,2,1,0:T(1,128)S(1)}, f32[4,3,1,1,128]{4,3,2,1,0:T(1,128)S(1)}, u32[]{:S(2)}, u32[]{:S(2)}) collective-permute-start(f32[4,3,1,1,128]{4,3,2,1,0:T(1,128)S(1)} %pad_maximum_fusion.10), channel_id=1, source_target_pairs={{1,0},{2,1},{3,2},{4,3},{5,4},{6,5},{7,6},{8,7},{9,8},{10,9},{11,1... | collective-permute-start | bytes 18440 | tf_op jit(solution)/shard_map/ppermute | solution.py:35
  77.0 5.4 %copy-start.43 = (f32[3]{0:T(128)S(1)}, f32[3]{0:T(128)}, u32[]{:S(2)}) copy-start(f32[3]{0:T(128)} %constant.533.clone) | copy-start | bytes 40
  77.0 5.7 %copy-start.11 = (f32[50,100]{1,0:T(8,128)S(1)}, f32[50,100]{1,0:T(8,128)}, u32[]{:S(2)}) copy-start(f32[50,100]{1,0:T(8,128)} %param.26) | copy-start | bytes 60004
  77.0 5.7 %copy-start.12 = (f32[25,50]{1,0:T(8,128)S(1)}, f32[25,50]{1,0:T(8,128)}, u32[]{:S(2)}) copy-start(f32[25,50]{1,0:T(8,128)} %param.24) | copy-start | bytes 15004
  77.0 5.7 %copy-start.21 = (f32[2,25]{1,0:T(2,128)S(1)}, f32[2,25]{1,0:T(2,128)}, u32[]{:S(2)}) copy-start(f32[2,25]{1,0:T(2,128)} %param.22) | copy-start | bytes 604
  77.0 5.7 %copy-start.22 = (f32[2,25]{1,0:T(2,128)S(1)}, f32[2,25]{1,0:T(2,128)}, u32[]{:S(2)}) copy-start(f32[2,25]{1,0:T(2,128)} %param.23) | copy-start | bytes 604
  77.0 5.7 %copy-start.23 = (f32[50]{0:T(128)S(1)}, f32[50]{0:T(128)}, u32[]{:S(2)}) copy-start(f32[50]{0:T(128)} %param.25) | copy-start | bytes 604
  77.0 5.7 %copy-start.44 = (f32[100]{0:T(128)S(1)}, f32[100]{0:T(128)}, u32[]{:S(2)}) copy-start(f32[100]{0:T(128)} %param.27) | copy-start | bytes 1204
  105.4 0.7 copy-start.3
  106.1 4.7 %copy-start.36 = (f32[240]{0:T(256)S(1)}, f32[240]{0:T(256)}, u32[]{:S(2)}) copy-start(f32[240]{0:T(256)} %param.29) | copy-start | bytes 2884
  109.7 2.7 copy-start.14
  109.7 2.7 copy-start.37
  109.7 3.3 %copy-start.15 = (f32[240,240]{1,0:T(8,128)S(1)}, f32[240,240]{1,0:T(8,128)}, u32[]{:S(2)}) copy-start(f32[240,240]{1,0:T(8,128)} %param.32) | copy-start | bytes 691204
  109.7 3.3 %copy-start.38 = (f32[240]{0:T(256)S(1)}, f32[240]{0:T(256)}, u32[]{:S(2)}) copy-start(f32[240]{0:T(256)} %param.33) | copy-start | bytes 2884
  110.8 2.8 %copy-start.16 = (f32[240,100]{0,1:T(8,128)S(1)}, f32[240,100]{0,1:T(8,128)}, u32[]{:S(2)}) copy-start(f32[240,100]{0,1:T(8,128)} %param.34) | copy-start | bytes 288004
  110.8 3.5 %copy-start.19 = (f32[3,1,1,1,128]{4,3,2,1,0:T(1,128)S(1)}, f32[3,1,1,1,128]{4,3,2,1,0:T(1,128)}, u32[]{:S(2)}) copy-start(f32[3,1,1,1,128]{4,3,2,1,0:T(1,128)} %param.19) | copy-start | bytes 4612
  110.9 3.5 %copy-start.41 = (f32[35]{0:T(128)S(1)}, f32[35]{0:T(128)}, u32[]{:S(2)}) copy-start(f32[35]{0:T(128)} %convert_add_fusion) | copy-start | bytes 424
  110.9 4.3 %copy-start.42 = (f32[19]{0:T(128)S(1)}, f32[19]{0:T(128)}, u32[]{:S(2)}) copy-start(f32[19]{0:T(128)} %convert_add_fusion.1) | copy-start | bytes 232
  110.9 4.4 %copy-start.34 = (f32[128]{0:T(128)S(1)}, f32[128]{0:T(128)}, u32[]{:S(2)}) copy-start(f32[128]{0:T(128)} %get-tuple-element.116) | copy-start | bytes 1540
  110.9 4.4 %copy-start.35 = (f32[128]{0:T(128)S(1)}, f32[128]{0:T(128)}, u32[]{:S(2)}) copy-start(f32[128]{0:T(128)} %get-tuple-element.117) | copy-start | bytes 1540
  110.9 4.4 %copy-start.45 = (f32[256]{0:T(256)S(1)}, f32[256]{0:T(256)}, u32[]{:S(2)}) copy-start(f32[256]{0:T(256)} %iota_convert_fusion) | copy-start | bytes 3076
  115.3 1.3 copy-start.39
  116.6 2.0 collective-permute-start.4
  116.6 8.2 %copy-start.29 = (pred[128]{0:T(512)(128)(4,1)}, pred[128]{0:T(512)(128)(4,1)S(1)}, u32[]{:S(2)}) copy-start(pred[128]{0:T(512)(128)(4,1)S(1)} %iota_compare_fusion) | copy-start | bytes 388
  116.7 7.3 %copy-start.9 = (f32[256,256]{1,0:T(8,128)S(1)}, f32[256,256]{1,0:T(8,128)}, u32[]{:S(2)}) copy-start(f32[256,256]{1,0:T(8,128)} %fusion.197) | copy-start | bytes 786436
  118.7 6.1 %copy-start.10 = (f32[256,256]{1,0:T(8,128)S(1)}, f32[256,256]{1,0:T(8,128)}, u32[]{:S(2)}) copy-start(f32[256,256]{1,0:T(8,128)} %fusion.196) | copy-start | bytes 786436
  118.7 5.3 %collective-permute-start.5 = (f32[3,32,256]{2,1,0:T(8,128)S(1)}, f32[3,32,256]{2,1,0:T(8,128)S(1)}, u32[]{:S(2)}, u32[]{:S(2)}) collective-permute-start(f32[3,32,256]{2,1,0:T(8,128)S(1)} %pad_maximum_fusion.7), channel_id=1, source_target_pairs={{0,15},{1,0},{2,1},{3,2},{4,3},{5,4},{6,5},{7,6},{8,7},{9,8},{10,9... | collective-permute-start | bytes 294920 | tf_op jit(solution)/shard_map/ppermute | solution.py:42
  126.9 26.4 %all-to-all-start = ((f32[2,128,512]{2,0,1:T(2,128)}), f32[2,128,512]{2,0,1:T(2,128)S(1)}, u32[]{:S(2)}, u32[]{:S(2)}) async-start(f32[2,128,512]{2,0,1:T(2,128)} %pad_maximum_fusion.1), calls=%async_computation | async-start | bytes 1048576 | tf_op jit(solution)/shard_map/all_to_all | solution.py:316
  141.0 32.6 %copy-start.30 = (pred[256]{0:T(512)(128)(4,1)}, pred[256]{0:T(512)(128)(4,1)S(1)}, u32[]{:S(2)}) copy-start(pred[256]{0:T(512)(128)(4,1)S(1)} %get-tuple-element.125) | copy-start | bytes 772
  141.1 32.6 %copy-start.32 = (pred[256]{0:T(512)(128)(4,1)}, pred[256]{0:T(512)(128)(4,1)S(1)}, u32[]{:S(2)}) copy-start(pred[256]{0:T(512)(128)(4,1)S(1)} %get-tuple-element.126) | copy-start | bytes 772
  156.3 5.0 %copy-start.8 = (f32[8,16,16,32]{3,2,1,0:T(8,128)S(1)}, f32[8,16,16,32]{3,2,1,0:T(8,128)}, u32[]{:S(2)}) copy-start(f32[8,16,16,32]{3,2,1,0:T(8,128)} %reshape.1387) | copy-start | bytes 786436
  170.0 3.7 %copy-start.26 = (f32[256]{0:T(256)S(1)}, f32[256]{0:T(256)}, u32[]{:S(2)}) copy-start(f32[256]{0:T(256)} %broadcast_add_fusion.1) | copy-start | bytes 3076
  171.5 2.7 copy-start.1
  173.5 4.2 %copy-start.4 = (f32[256,1]{1,0:T(8,128)}, f32[256,1]{1,0:T(8,128)S(1)}, u32[]{:S(2)}) copy-start(f32[256,1]{1,0:T(8,128)S(1)} %fusion.150) | copy-start | bytes 3076
  173.7 4.1 %copy-start.6 = (f32[256,1]{1,0:T(8,128)}, f32[256,1]{1,0:T(8,128)S(1)}, u32[]{:S(2)}) copy-start(f32[256,1]{1,0:T(8,128)S(1)} %fusion.151) | copy-start | bytes 3076
  179.6 7.0 %copy-start.13 = (f32[16,16,256,1]{2,1,0,3:T(8,128)}, f32[16,16,256,1]{2,1,0,3:T(8,128)S(1)}, u32[]{:S(2)}) copy-start(f32[16,16,256,1]{2,1,0,3:T(8,128)S(1)} %fusion.25) | copy-start | bytes 786436
  196.6 18.2 %all-to-all-start.1 = ((f32[2,128,512]{2,0,1:T(2,128)}), f32[2,128,512]{2,0,1:T(2,128)S(1)}, u32[]{:S(2)}, u32[]{:S(2)}) async-start(f32[2,128,512]{2,0,1:T(2,128)} %pad_maximum_fusion.2), calls=%async_computation.1 | async-start | bytes 1048576 | tf_op jit(solution)/shard_map/all_to_all | solution.py:355
  216.0 11.1 %copy-start.2 = (f32[256,256]{1,0:T(8,128)S(1)}, f32[256,256]{1,0:T(8,128)}, u32[]{:S(2)}) copy-start(f32[256,256]{1,0:T(8,128)} %copy-done.1) | copy-start | bytes 786436
  216.0 11.1 %copy-start.5 = (f32[256,1]{1,0:T(8,128)S(1)}, f32[256,1]{1,0:T(8,128)}, u32[]{:S(2)}) copy-start(f32[256,1]{1,0:T(8,128)} %copy-done.4) | copy-start | bytes 3076
  216.0 11.1 %copy-start.7 = (f32[256,1]{1,0:T(8,128)S(1)}, f32[256,1]{1,0:T(8,128)}, u32[]{:S(2)}) copy-start(f32[256,1]{1,0:T(8,128)} %copy-done.6) | copy-start | bytes 3076
  216.0 11.1 %copy-start.27 = (f32[256]{0:T(256)S(1)}, f32[256]{0:T(256)}, u32[]{:S(2)}) copy-start(f32[256]{0:T(256)} %broadcast_add_fusion.1) | copy-start | bytes 3076
  217.9 9.2 %copy-start.31 = (pred[256]{0:T(512)(128)(4,1)S(1)}, pred[256]{0:T(512)(128)(4,1)}, u32[]{:S(2)}) copy-start(pred[256]{0:T(512)(128)(4,1)} %copy-done.30) | copy-start | bytes 772
  217.9 9.2 %copy-start.33 = (pred[256]{0:T(512)(128)(4,1)S(1)}, pred[256]{0:T(512)(128)(4,1)}, u32[]{:S(2)}) copy-start(pred[256]{0:T(512)(128)(4,1)} %copy-done.32) | copy-start | bytes 772
  221.1 4.7 %collective-permute-start.6 = (f32[3,32,256]{2,1,0:T(8,128)S(1)}, f32[3,32,256]{2,1,0:T(8,128)S(1)}, u32[]{:S(2)}, u32[]{:S(2)}) collective-permute-start(f32[3,32,256]{2,1,0:T(8,128)S(1)} %slice.224), channel_id=1, source_target_pairs={{0,1},{1,2},{2,3},{3,4},{4,5},{5,6},{6,7},{7,8},{8,9},{9,10},{10,1... | collective-permute-start | bytes 294920 | tf_op jit(solution)/shard_map/ppermute | solution.py:42
  225.8 0.6 copy-start.17
  227.1 38.2 %collective-permute-start.7 = (f32[19,3,256]{2,1,0:T(4,128)}, f32[19,3,256]{2,1,0:T(4,128)}, u32[]{:S(2)}, u32[]{:S(2)}) collective-permute-start(f32[19,3,256]{2,1,0:T(4,128)} %pad_maximum_fusion.8), channel_id=1, source_target_pairs={{0,16},{16,32},{32,48},{48,64},{64,80},{80,96},{96,112},{112,0},{1... | collective-permute-start | bytes 175112 | tf_op jit(solution)/shard_map/ppermute | solution.py:42
  265.3 2.4 copy-start.18
  265.3 2.4 copy-start.20
  265.3 2.4 copy-start.40
  265.3 2.4 copy-start.46
  267.7 2.8 %copy-start.25 = (f32[128]{0:T(128)S(1)}, f32[128]{0:T(128)}, u32[]{:S(2)}) copy-start(f32[128]{0:T(128)} %copy-done.24) | copy-start | bytes 1540
where the time goes:
time: 277 us; the launch traced here: 273 us
  local copies, waits for them, and re-layouts  76.3 us (28%)
  matrix products  70 us (25%)
  waiting for transfers between devices  36.6 us (13%)
  blocking collectives  35.5 us (13%)
  starting transfers between devices  26.1 us (9%)
  other arithmetic  23.4 us (8%)
  between operations  4.22 us (2%)
    gather x2, local copies, waits for them, and re-layouts, local(): nearby = jnp.take(ghost_table, source, axis=1)  60.1 us
    psum x4, blocking collectives, over_axes(): return functools.reduce(lax.psum, axes, x)  35.5 us
    all_to_all x2, waiting for transfers between devices, local(): lax.all_to_all(outgoing, WIDE_NARROW, split_axis=1, concat_axis=1, tiled=...  24.1 us
    all_to_all x2, starting transfers between devices, local(): lax.all_to_all(outgoing, WIDE_NARROW, split_axis=1, concat_axis=1, tiled=...  19.8 us
    dot_general x2, matrix products, environment(): jnp.einsum('pbn,dbn->pdb', radial, third_layer, precision=largest_value)  11.5 us
    ppermute x4, waiting for transfers between devices, shifted(): lax.ppermute(x, axis, [(i, (i + by) % length) for i in range(length)])  10.7 us
    dot_general x4, matrix products, rotate(): jnp.einsum(pattern, real_part, sin_table, precision=largest_value)  8.97 us
    dot_general x4, matrix products, rotate(): jnp.einsum(pattern, real_part, cos_table, precision=largest_value)  8.37 us
  transfers between devices with their start and end apart: 10, of which 7 were waited for; matrix products, arithmetic and copies ran while one was open for 5% of the time, Pallas kernels for 0%

commit v1 on v0

v1 whole, which is shorter than its diff:
```python
import functools
import math

import jax
import jax.numpy as jnp
import numpy as np
from jax import lax
from jax.experimental import pallas as pl
from jax.experimental.pallas import tpu as pltpu
from jax.sharding import PartitionSpec as P

NW, NN = 8, 16
ND = NW * NN
CX, CY, CZ = 32, 256, 16
TX, TZ = 40, 19
TILE = 768
FOLD = 640
MODES = 512
ATOMS = 128
F32 = jnp.float32
BF16 = jnp.bfloat16
MESH = pl.DeviceIdType.MESH
HIGHEST = lax.Precision.HIGHEST
NT = (((1,), (1,)), ((), ()))
NNN = (((1,), (0,)), ((), ()))


def split(x):
    high = x.astype(BF16)
    return high, (x - high.astype(F32)).astype(BF16)


def mm(a, b, dims=NNN):
    return lax.dot_general(a, b, dims, preferred_element_type=F32)


def mm3(a, b, dims=NNN):
    return mm(a[0], b[0], dims) + mm(a[0], b[1], dims) + mm(a[1], b[0], dims)


def exact(a, b, dims=NNN):
    return lax.dot_general(a, b, dims, precision=HIGHEST, preferred_element_type=F32)


def iota(shape, dim):
    return lax.broadcasted_iota(jnp.int32, shape, dim)


def spline(offset):
    square = offset * offset
    cube = square * offset
    remain = 4.0 - offset
    one = cube * (1.0 / 6.0)
    two = (-3.0 * cube + 12.0 * square - 12.0 * offset + 4.0) * (1.0 / 6.0)
    three = (3.0 * cube - 24.0 * square + 60.0 * offset - 44.0) * (1.0 / 6.0)
    four = remain * remain * remain * (1.0 / 6.0)
    value = jnp.where(
        offset < 1.0, one, jnp.where(offset < 2.0, two, jnp.where(offset < 3.0, three, four))
    )
    return jnp.where((offset >= 0.0) & (offset < 4.0), value, 0.0)


def slope(offset):
    square = offset * offset
    remain = 4.0 - offset
    one = square * 0.5
    two = (-9.0 * square + 24.0 * offset - 12.0) * (1.0 / 6.0)
    three = (9.0 * square - 48.0 * offset + 60.0) * (1.0 / 6.0)
    four = -0.5 * remain * remain
    value = jnp.where(
        offset < 1.0, one, jnp.where(offset < 2.0, two, jnp.where(offset < 3.0, three, four))
    )
    return jnp.where((offset >= 0.0) & (offset < 4.0), value, 0.0)


def halo_kernel(own_ref, ghost_ref, send_sem, recv_sem):
    wide = lax.axis_index("wide")
    narrow = lax.axis_index("narrow")
    steps = [(sx, sz) for sx in range(3) for sz in range(3) if (sx, sz) != (1, 1)]
    barrier = pltpu.get_barrier_semaphore()

    def device(sx, sz):
        return (lax.rem(wide + (NW + 1 - sx), NW), lax.rem(narrow + (NN + 1 - sz), NN))

    for sx, sz in steps:
        pl.semaphore_signal(barrier, inc=1, device_id=device(sx, sz), device_id_type=MESH)
    pl.semaphore_wait(barrier, len(steps))
    copies = []
    for at, (sx, sz) in enumerate(steps):
        copy = pltpu.make_async_remote_copy(
            src_ref=own_ref,
            dst_ref=ghost_ref.at[sx * 3 + sz],
            send_sem=send_sem.at[at],
            recv_sem=recv_sem.at[at],
            device_id=device(sx, sz),
            device_id_type=MESH,
        )
        copy.start()
        copies.append(copy)
    ghost_ref[4] = own_ref[...]
    for copy in copies:
        copy.wait()


def halo(own):
    return pl.pallas_call(
        halo_kernel,
        out_shape=jax.ShapeDtypeStruct((9, 8, ATOMS), F32),
        in_specs=[pl.BlockSpec(memory_space=pltpu.VMEM)],
        out_specs=pl.BlockSpec(memory_space=pltpu.VMEM),
        scratch_shapes=[pltpu.SemaphoreType.DMA((8,)), pltpu.SemaphoreType.DMA((8,))],
        compiler_params=pltpu.CompilerParams(collective_id=0, has_side_effects=True),
        name="halo",
    )(own)


def spread_rows(rows, count):
    r = iota((rows, count), 0)
    c = iota((rows, count), 1)
    i = r & 31
    return jnp.where((i < 25) & (c == (r >> 5) * 25 + i), 1.0, 0.0).astype(F32)


def net_kernel(
    ghost_ref,
    near_ref,
    e1w_ref,
    e1b_ref,
    e2w_ref,
    e2b_ref,
    e3w_ref,
    e3b_ref,
    f1w_ref,
    f1b_ref,
    f2w_ref,
    f2b_ref,
    f3w_ref,
    f3b_ref,
    fow_ref,
    dip_ref,
    table_ref,
    own_ref,
    mat_ref,
    left_ref,
    right_ref,
):
    extent = (float(CX), float(CY), float(CZ))
    for k in range(9):
        shift = (float(k // 3 - 1), 0.0, float(k % 3 - 1))
        for c in range(3):
            table_ref[k * 4 + c] = jnp.broadcast_to(ghost_ref[k, c : c + 1, :] + shift[c], (8, ATOMS))
        table_ref[k * 4 + 3] = jnp.broadcast_to(ghost_ref[k, 3:4, :], (8, ATOMS))
    for c in range(3):
        own_ref[c] = jnp.broadcast_to(ghost_ref[4, c : c + 1, :], (ATOMS, ATOMS)).T

    pick1 = spread_rows(32, 25)
    pick2 = spread_rows(64, 50)
    pick3 = spread_rows(128, 100)

    def column(pick, row):
        return exact(pick, jnp.broadcast_to(row, (ATOMS, row.shape[1])), NT)

    w_oxygen = column(pick1, e1w_ref[0:1, :])
    w_hydrogen = column(pick1, e1w_ref[1:2, :])
    b_oxygen = column(pick1, e1b_ref[0:1, :])
    b_hydrogen = column(pick1, e1b_ref[1:2, :])
    bias2 = column(pick2, e2b_ref[...])
    bias3 = column(pick3, e3b_ref[...])
    w2 = exact(pick2, exact(pick1, e2w_ref[...]), NT)
    w3 = exact(pick3, exact(pick2, e3w_ref[...]), NT)
    w2_high, w2_low = split(w2)
    w3_high, w3_low = split(w3)
    w2_all = jnp.concatenate([w2_high, w2_high, w2_low], axis=1)
    w3_all = jnp.concatenate([w3_high, w3_high, w3_low], axis=1)
    bias2 = jnp.concatenate([bias2] * 8, axis=1)
    bias3 = jnp.concatenate([bias3] * 8, axis=1)
    sublane = iota((8, ATOMS), 0)

    def group(g, carry):
        rows = pl.ds(pl.multiple_of(g * 8, 8), 8)
        code = near_ref[rows, :]
        slot = code & 127
        offset = code >> 7
        brick = (offset * 11) >> 5
        step_y = (offset - 3 * brick - 1).astype(F32)
        parts = [jnp.zeros((8, ATOMS), F32)] * 4
        for k in range(9):
            here = brick == k
            for c in range(4):
                found = jnp.take_along_axis(table_ref[k * 4 + c], slot, axis=1)
                parts[c] = jnp.where(here, found, parts[c])
        parts[1] = parts[1] + step_y
        scaled = [(parts[c] - own_ref[c, rows, :]) * (extent[c] / 24.0) for c in range(3)]
        square = scaled[0] * scaled[0] + scaled[1] * scaled[1] + scaled[2] * scaled[2]
        smooth = 1.0 / (1.0 + square)
        kind = parts[3]
        pieces = []
        for b in range(8):
            s = jnp.broadcast_to(smooth[b : b + 1, :], (32, ATOMS))
            h = jnp.broadcast_to(kind[b : b + 1, :], (32, ATOMS)) > 0.5
            pieces.append(
                jnp.where(h, w_hydrogen, w_oxygen) * s + jnp.where(h, b_hydrogen, b_oxygen)
            )
        one = jnp.tanh(jnp.concatenate(pieces, axis=1))
        high, low = split(one)
        two = jnp.tanh(mm(w2_all, jnp.concatenate([high, low, high], axis=0)) + bias2)
        two = two + jnp.concatenate([one, one], axis=0)
        high, low = split(two)
        three = jnp.tanh(mm(w3_all, jnp.concatenate([high, low, high], axis=0)) + bias3)
        three = three + jnp.concatenate([two, two], axis=0)
        high, low = split(three)
        scale = smooth * (1.0 / 128.0)
        radial = [scale] + [scale * scaled[c] for c in range(3)]
        blocks = []
        for b in range(8):
            mine = sublane == b
            blocks.append(jnp.concatenate([jnp.where(mine, r, 0.0) for r in radial], axis=0))
        radial = jnp.concatenate(blocks, axis=1)
        r_high, r_low = split(radial)
        found = mm(r_high, high, NT) + mm(r_high, low, NT) + mm(r_low, high, NT)
        for p in range(4):
            mat_ref[p, rows, :] = found[p * 8 : (p + 1) * 8]
        return carry

    lax.fori_loop(0, ATOMS // 8, group, 0)

    matrix = [exact(mat_ref[p], pick3) for p in range(4)]
    left_ref[...] = f1w_ref[:, :128]
    right_ref[...] = jnp.concatenate([f1w_ref[:, 128:], jnp.zeros((1600, 16), F32)], axis=1)
    hidden = jnp.zeros((ATOMS, 256), F32)
    for e in range(16):
        entry = matrix[0] * matrix[0][:, e : e + 1]
        for p in range(1, 4):
            entry = entry + matrix[p] * matrix[p][:, e : e + 1]
        weight = jnp.concatenate(
            [left_ref[pl.ds(e, 100, stride=16), :], right_ref[pl.ds(e, 100, stride=16), :]], axis=1
        )
        hidden = hidden + mm3(split(entry), split(weight))
    hidden = hidden[:, :240]
    hidden = jnp.tanh(hidden + f1b_ref[...])
    hidden = hidden + jnp.tanh(mm3(split(hidden), split(f2w_ref[...])) + f2b_ref[...])
    hidden = hidden + jnp.tanh(mm3(split(hidden), split(f3w_ref[...])) + f3b_ref[...])
    coeffs = mm3(split(hidden), split(fow_ref[...]))
    lane = iota((ATOMS, ATOMS), 1)
    result = jnp.zeros((ATOMS, ATOMS), F32)
    for c in range(3):
        total = jnp.sum(coeffs * matrix[1 + c], axis=1, keepdims=True)
        result = jnp.where(lane == c, total, result)
    dip_ref[...] = result.T[:8]


def net(ghosts, neighbours, weights):
    vmem = pl.BlockSpec(memory_space=pltpu.VMEM)
    return pl.pallas_call(
        net_kernel,
        out_shape=jax.ShapeDtypeStruct((8, ATOMS), F32),
        in_specs=[vmem] * (2 + len(weights)),
        out_specs=vmem,
        scratch_shapes=[
            pltpu.VMEM((36, 8, ATOMS), F32),
            pltpu.VMEM((3, ATOMS, ATOMS), F32),
            pltpu.VMEM((4, ATOMS, ATOMS), F32),
            pltpu.VMEM((1600, ATOMS), F32),
            pltpu.VMEM((1600, ATOMS), F32),
        ],
        compiler_params=pltpu.CompilerParams(vmem_limit_bytes=32 << 20),
        name="net",
    )(ghosts, neighbours, *weights)


def np_split(x):
    x = np.asarray(x, np.float32)
    high = x.astype(jnp.bfloat16)
    low = (x - high.astype(np.float32)).astype(jnp.bfloat16)
    return np.stack([high, low])


@functools.lru_cache(None)
def tables():
    m = np.arange(128)[:, None]
    y = np.arange(CY)[None, :]
    angle = 2 * np.pi * (m * y % CY) / CY
    lower = -np.sin(angle)
    lower[0] = 1 - 2 * (y[0] % 2)
    dft_y = np_split(np.concatenate([np.cos(angle), lower]))
    j, k = np.divmod(np.arange(ND), NN)
    phi = 2 * np.pi * ((2 * j[:, None] * j[None] + k[:, None] * k[None]) % 16) / 16
    cos, sin = np.cos(phi), np.sin(phi)
    dft_b = np_split(np.block([[cos, sin], [-sin, cos]]))
    z, x = np.divmod(np.arange(TILE), TX)
    turn = 2 * np.pi * ((j[:, None] * (x - 3)[None] + k[:, None] * (z - 3)[None]) % 256) / 256
    twiddle = np.stack([np.cos(turn), np.sin(turn)]).astype(np.float32)
    v, u = np.divmod(np.arange(MODES), 32)
    ax = 2 * np.pi * ((np.arange(TX)[:, None] - 3) * u[None] % 32) / 32
    az = 2 * np.pi * ((np.arange(16)[:, None] - 3) * v[None] % 16) / 16
    fac_x = np.stack([np.cos(ax), np.sin(ax)]).astype(np.float32)
    fac_z = np.stack([np.cos(az), np.sin(az)]).astype(np.float32)

    def fold(i, n):
        return np.where(2 * i >= n, i - n, i) / n

    def modulus(i, n):
        return 36.0 / (4 + 2 * np.cos(2 * np.pi * i / n)) ** 2

    def decay(f):
        return np.exp(-np.pi**2 * f * f / 0.81)

    mx = j[:, None] + 8 * u[None]
    mz = k[:, None] + 16 * v[None]
    fx, fz = fold(mx, 256), fold(mz, 256)
    scale = 0.25 / (np.pi * 256.0**3)
    plane = scale * decay(fx) * decay(fz) * modulus(mx, 256) * modulus(mz, 256)
    green = np.stack([plane, fx * fx + fz * fz]).astype(np.float32)
    my = np.arange(129)
    fy = fold(my, 256)
    column = np.stack([decay(fy) * modulus(my, 256), fy * fy]).astype(np.float32)
    return dft_y, dft_b, twiddle, fac_x, fac_z, green, column


def long_kernel(
    own_ref,
    dip_ref,
    dft_y_ref,
    dft_b_ref,
    twiddle_ref,
    fac_x_ref,
    fac_z_ref,
    green_ref,
    column_ref,
    dipole_ref,
    atom_ref,
    centroid_ref,
    energy_ref,
    mix_ref,
    wave_ref,
    tab_ref,
    out_one,
    in_one,
    out_two,
    in_two,
    send_sem,
    recv_sem,
):
    wide = lax.axis_index("wide")
    narrow = lax.axis_index("narrow")
    me = wide * NN + narrow
    barrier = pltpu.get_barrier_semaphore()

    def peer(d):
        at = lax.rem(me + d, ND)
        return at, (at // NN, lax.rem(at, NN))

    def greet(d, carry):
        pl.semaphore_signal(barrier, inc=1, device_id=peer(d)[1], device_id_type=MESH)
        return carry

    lax.fori_loop(1, ND, greet, 0)

    kind = own_ref[3:4, :]
    oxygen = 1.0 - kind
    dip = dip_ref[...]
    dipole_ref[...] = dip * oxygen
    shift = 0.5 * jnp.tanh(dip)

    def sites(c, extent):
        atom = own_ref[c : c + 1, :] * float(extent)
        return jnp.concatenate([atom, atom + shift[c : c + 1, :]], axis=1)

    charge = jnp.concatenate([6.0 * oxygen + kind, -8.0 * oxygen], axis=1)
    off_x = sites(0, CX) - (iota((TX, 256), 0).astype(F32) - 3.0)
    off_z = sites(2, CZ) - (iota((24, 256), 0).astype(F32) - 3.0)
    off_y = sites(1, CY) - iota((CY, 256), 0).astype(F32)
    off_y = jnp.where(off_y < 0.0, off_y + float(CY), off_y)
    wx, sx = spline(off_x), slope(off_x)
    wz, sz = spline(off_z), slope(off_z)
    wave = mm3(
        (dft_y_ref[0], dft_y_ref[1]),
        split(jnp.concatenate([spline(off_y), slope(off_y)], axis=1)),
    )
    wave_ref[...] = wave
    rest = jnp.zeros((TILE - TX * TZ, 256), F32)
    for at, (left, right) in enumerate(((wz, wx), (wz, sx), (sz, wx))):
        full = jnp.concatenate([left[z : z + 1, :] * right for z in range(TZ)] + [rest], axis=0)
        high, low = split(full)
        mix_ref[0, :, at * 256 : (at + 1) * 256] = high
        mix_ref[1, :, at * 256 : (at + 1) * 256] = low
    spread = mm3(
        split(wave[:, :256] * charge), (mix_ref[0, :, :256], mix_ref[1, :, :256]), NT
    )
    for part in range(2):
        for t in range(6):
            out_one[:, part * 6 + t, :] = spread[part * 128 : (part + 1) * 128, t * 128 : (t + 1) * 128]

    pl.semaphore_wait(barrier, ND - 1)

    def exchange(out_ref, in_ref, s):
        def one(d, carry):
            at, device = peer(d)
            pltpu.make_async_remote_copy(
                src_ref=out_ref.at[at],
                dst_ref=in_ref.at[me],
                send_sem=send_sem.at[s],
                recv_sem=recv_sem.at[s],
                device_id=device,
                device_id_type=MESH,
            ).start()
            return carry

        lax.fori_loop(1, ND, one, 0)
        in_ref[me] = out_ref[me]

    def settle(out_ref, in_ref, s):
        whole = pltpu.make_async_remote_copy(
            src_ref=out_ref.at[pl.ds(0, ND - 1)],
            dst_ref=in_ref.at[pl.ds(0, ND - 1)],
            send_sem=send_sem.at[s],
            recv_sem=recv_sem.at[s],
            device_id=peer(1)[1],
            device_id_type=MESH,
        )
        whole.wait_send()
        whole.wait_recv()

    exchange(out_one, in_one, 0)

    def build(z, carry):
        cz = fac_z_ref[0, pl.ds(z, 1), :]
        zz = fac_z_ref[1, pl.ds(z, 1), :]
        cx, xx = fac_x_ref[0], fac_x_ref[1]
        rows = pl.ds(pl.multiple_of(z * TX, 8), TX)
        tab_ref[0, rows, :] = cx * cz - xx * zz
        tab_ref[1, rows, :] = xx * cz + cx * zz
        return carry

    lax.fori_loop(0, 16, build, 0)
    cos_e = split(tab_ref[0])
    sin_e = split(tab_ref[1])

    settle(out_one, in_one, 0)

    def gathered(in_ref):
        return jnp.concatenate(
            [
                jnp.concatenate([in_ref[:, part * 6 + t, :] for t in range(6)], axis=1)
                for part in range(2)
            ],
            axis=0,
        )

    tiles = gathered(in_one)
    bricks = mm3((dft_b_ref[0], dft_b_ref[1]), split(tiles))
    real, imag = bricks[:128], bricks[128:]
    cos_t, sin_t = twiddle_ref[0], twiddle_ref[1]
    turned = jnp.concatenate(
        [real * cos_t + imag * sin_t, imag * cos_t - real * sin_t], axis=0
    )
    turned = jnp.concatenate(
        [turned[:, :128] + turned[:, FOLD:], turned[:, 128:FOLD]], axis=1
    )
    turned = split(turned)
    by_cos = mm3(turned, cos_e)
    by_sin = mm3(turned, sin_e)
    real = by_cos[:128] + by_sin[128:]
    imag = by_cos[128:] - by_sin[:128]

    def influence(at, weight):
        total = green_ref[1] + column_ref[1, at]
        inverse = jnp.where(total == 0.0, 0.0, 1.0 / jnp.where(total == 0.0, 1.0, total))
        return green_ref[0] * (inverse * (column_ref[0, at] * weight))

    first = me == 0
    weight = jnp.where(first, 1.0, 2.0)
    green_a = influence(me, weight)
    green_b = influence(jnp.where(first, 128, me), weight)
    modes = split(
        jnp.concatenate(
            [green_a * real, green_a * imag, green_b * real, green_b * imag], axis=0
        )
    )
    by_cos = mm3(modes, cos_e, NT)
    by_sin = mm3(modes, sin_e, NT)

    def widen(x):
        return jnp.concatenate([x, x[:, :128]], axis=1)

    def back(at):
        real = widen(by_cos[at : at + 128] - by_sin[at + 128 : at + 256])
        imag = widen(by_sin[at : at + 128] + by_cos[at + 128 : at + 256])
        return real * cos_t - imag * sin_t, imag * cos_t + real * sin_t

    real_a, imag_a = back(0)
    real_b, imag_b = back(256)
    field_r = mm3(
        (dft_b_ref[0, :128], dft_b_ref[1, :128]),
        split(jnp.concatenate([real_a, -imag_a], axis=0)),
    )
    field_i = mm3(
        (dft_b_ref[0, 128:], dft_b_ref[1, 128:]),
        split(jnp.concatenate([-real_b, imag_b], axis=0)),
    )
    partial = jnp.sum(tiles[:128] * field_r + tiles[128:] * field_i, keepdims=True)
    partial = partial * (0.5 / (ND * ATOMS))
    lane = iota((ND, 128), 1)
    for t in range(6):
        piece = field_r[:, t * 128 : (t + 1) * 128]
        if t == 5:
            piece = jnp.where(lane == 127, partial, piece)
        out_two[:, t, :] = piece
        out_two[:, 6 + t, :] = field_i[:, t * 128 : (t + 1) * 128]

    exchange(out_two, in_two, 1)
    settle(out_two, in_two, 1)

    planes = gathered(in_two)
    inner = mm3(split(planes), (mix_ref[0], mix_ref[1]))
    wave = wave_ref[:, :256]
    wave_slope = wave_ref[:, 256:]
    rows = [
        jnp.sum(wave * inner[:, :256], axis=0, keepdims=True),
        -jnp.sum(wave * inner[:, 256:512], axis=0, keepdims=True),
        -jnp.sum(wave_slope * inner[:, :256], axis=0, keepdims=True),
        -jnp.sum(wave * inner[:, 512:], axis=0, keepdims=True),
    ]
    for c in range(4):
        atom_ref[c : c + 1, :] = rows[c][:, :128]
        centroid_ref[c : c + 1, :] = rows[c][:, 128:] * oxygen
    energy_ref[...] = jnp.broadcast_to(
        jnp.sum(planes[:128, TILE - 1 : TILE], axis=0, keepdims=True), (8, 128)
    )


def long_range(own, dip):
    vmem = pl.BlockSpec(memory_space=pltpu.VMEM)
    smem = pl.BlockSpec(memory_space=pltpu.SMEM)
    consts = [jnp.asarray(t) for t in tables()]
    return pl.pallas_call(
        long_kernel,
        out_shape=(
            jax.ShapeDtypeStruct((8, ATOMS), F32),
            jax.ShapeDtypeStruct((4, ATOMS), F32),
            jax.ShapeDtypeStruct((4, ATOMS), F32),
            jax.ShapeDtypeStruct((8, ATOMS), F32),
        ),
        in_specs=[vmem] * 8 + [smem],
        out_specs=(vmem,) * 4,
        scratch_shapes=[
            pltpu.VMEM((2, TILE, TILE), BF16),
            pltpu.VMEM((CY, 512), F32),
            pltpu.VMEM((2, FOLD, MODES), F32),
            pltpu.VMEM((ND, 12, 128), F32),
            pltpu.VMEM((ND, 12, 128), F32),
            pltpu.VMEM((ND, 12, 128), F32),
            pltpu.VMEM((ND, 12, 128), F32),
            pltpu.SemaphoreType.DMA((2,)),
            pltpu.SemaphoreType.DMA((2,)),
        ],
        compiler_params=pltpu.CompilerParams(
            collective_id=1, has_side_effects=True, vmem_limit_bytes=50 << 20
        ),
        name="long_range",
    )(own, dip, *consts)


def local(positions, species, neighbours, *weights):
    own = jnp.concatenate(
        [
            positions.reshape(3, ATOMS),
            species.reshape(1, ATOMS).astype(F32),
            jnp.zeros((4, ATOMS), F32),
        ],
        axis=0,
    )
    ghosts = halo(own)
    weights = [w.reshape(1, -1) if w.ndim == 1 else w for w in weights]
    dip = net(ghosts, neighbours.reshape(ATOMS, ATOMS), weights)
    dipole, atom, centroid, energy = long_range(own, dip)
    return (
        dipole[:3].reshape(3, 1, 1, 1, ATOMS),
        atom.reshape(4, 1, 1, 1, ATOMS),
        centroid.reshape(4, 1, 1, 1, ATOMS),
        energy[0, 0],
    )


def solution(mesh):
    return jax.shard_map(
        local,
        mesh=mesh,
        in_specs=(
            P(None, "wide", "narrow", None, None),
            P("wide", "narrow", None, None),
            P("wide", "narrow", None, None, None),
        )
        + (P(),) * 13,
        out_specs=(
            P(None, "wide", "narrow", None, None),
            P(None, "wide", "narrow", None, None),
            P(None, "wide", "narrow", None, None),
            P(),
        ),
        check_vma=False,
    )
```

time: 277 us -> 85.8 us (0.31)
  the two profiles are of different devices: /device:TPU:34 before, /device:TPU:1 now
where the time goes in v1:
time: 85.8 us; the launch traced here: 85.5 us
  Pallas kernels  77.2 us (90%)
  local copies, waits for them, and re-layouts  6.07 us (7%)
  other arithmetic  1.31 us (2%)
  between operations  0.98 us (1%)
    pallas_call x1, Pallas kernels, long_range(): pl.pallas_call(long_kernel, out_shape=(jax.ShapeDtypeStruct((8, ATOMS), F...  45.8 us
    pallas_call x1, Pallas kernels, net(): pl.pallas_call(net_kernel, out_shape=jax.ShapeDtypeStruct((8, ATOMS), F32...  18.4 us
    pallas_call x1, Pallas kernels, halo(): pl.pallas_call(halo_kernel, out_shape=jax.ShapeDtypeStruct((9, 8, ATOMS),...  13.1 us
    unnamed x48, local copies, waits for them, and re-layouts  5.47 us

profile of v1, /device:TPU:1, one launch (start us, length us, event | category | flops | bytes accessed | tf_op | source)
XLA Modules:
  0.0 85.5 jit_solution(14060168808475192540)
XLA Ops:
  0.6 0.7 convert_bitcast_fusion
  1.3 0.1 pad.2.clone
  1.4 0.7 copy.34
  2.0 0.7 maximum_maximum_fusion.own_ref
  2.7 13.1 %halo.1.ghost_ref = f32[9,8,128]{2,1,0:T(8,128)} custom-call(f32[8,128]{1,0:T(8,128)} %maximum_maximum_fusion.own_ref), custom_call_target="tpu_custom_call" | custom-call | tf_op jit(solution)/shard_map/halo/pallas_call | solution.py:106
  15.8 1.0 %copy.28.fow_ref = f32[240,100]{1,0:T(8,128)S(1)} copy(f32[240,100]{0,1:T(8,128)} %param.38) | data formatting | bytes 192000 | tf_op args[15]
  16.8 0.0 copy-start.4
  16.8 0.0 copy-start.5
  16.8 0.0 copy-start.7
  16.8 0.0 copy-start.8
  16.8 0.0 copy-start.11
  16.8 0.0 copy-start.12
  16.8 0.0 copy-start.14
  16.8 0.0 copy-start.15
  16.9 0.0 copy-start.16
  16.9 0.0 copy-start.17
  16.9 0.0 copy-start.18
  16.9 0.0 copy-start.19
  16.9 0.0 copy-start.20
  16.9 1.9 %copy.27.f1w_ref = f32[1600,240]{1,0:T(8,128)S(1)} copy(f32[1600,240]{0,1:T(8,128)} %param.32) | data formatting | bytes 3072000 | tf_op args[9]
  18.9 0.0 copy-done.4
  18.9 0.0 copy-done.5
  18.9 0.0 copy-done.7
  18.9 0.0 copy-done.8
  18.9 0.0 copy-done.11
  18.9 0.0 copy-done.12
  18.9 0.0 copy-done.14
  18.9 0.0 copy-done.15
  19.0 0.0 copy-done.16
  19.0 0.0 copy-done.17
  19.0 0.0 copy-done.18
  19.0 0.0 copy-done.19
  19.0 0.0 copy-done.20
  19.0 0.0 copy-start
  19.0 0.0 copy-start.1
  19.0 0.0 copy-start.2
  19.0 0.0 copy-start.3
  19.1 0.0 copy-start.6
  19.1 0.0 copy-start.9
  19.1 0.0 copy-start.10
  19.1 0.0 copy-start.13
  19.1 18.4 %net.1.dip_ref = f32[8,128]{1,0:T(8,128)S(1)} custom-call(f32[9,8,128]{2,1,0:T(8,128)S(1)} %copy-done.7, s32[128,128]{1,0:T(8,128)S(1)} %bitcast.20, f32[2,25]{1,0:T(2,128)S(1)} %copy-done.14, f32[2,25]{1,0:T(2,128)S(1)} %copy-done.15, f32[25,50]{1,0:T(8,128)S(1)} %copy-done.12, f32[1,50]{1,0:T(1,128)S(1)} %bitcast.26, f32[50,100]{1,0:T(8,128)S(1)} %copy-done.11, ...), custom_call_target="tpu_custom_call" | custom-call | tf_op jit(solution)/shard_map/net/pallas_call | solution.py:254
  37.5 0.0 copy-done
  37.5 0.0 copy-done.1
  37.5 0.0 copy-done.2
  37.5 0.0 copy-done.3
  37.5 0.0 copy-done.6
  37.5 0.0 copy-done.9
  37.5 0.0 copy-done.10
  37.5 0.0 copy-done.13
  37.5 45.8 %long_range.1 = (f32[8,128]{1,0:T(8,128)S(1)}, f32[4,128]{1,0:T(4,128)S(1)}, f32[4,128]{1,0:T(4,128)S(1)}, f32[8,128]{1,0:T(8,128)S(1)}) custom-call(f32[8,128]{1,0:T(8,128)S(1)} %copy-done.10, f32[8,128]{1,0:T(8,128)S(1)} %net.1.dip_ref, bf16[2,256,256]{2,1,0:T(8,128)(2,1)S(1)} %copy-done.3, bf16[2,256,256]{2,1,0:T(8,128)(2,1)S(1)} %copy-done.2, ...), custom_call_target="tpu_custom_call" | custom-call | tf_op jit(solution)/shard_map/long_range/pallas_call | solution.py:536
  83.3 0.5 slice.7
  83.8 0.6 copy.29
  84.4 0.6 copy.37
  85.0 0.6 copy.38
  (2 shorter events, 0.0 us)
Async XLA Ops:
  16.8 2.1 %copy-start.4 = (f32[240,240]{1,0:T(8,128)S(1)}, f32[240,240]{1,0:T(8,128)}, u32[]{:S(2)}) copy-start(f32[240,240]{1,0:T(8,128)} %f2w_ref.1) | copy-start | bytes 691204
  16.8 2.1 %copy-start.5 = (f32[240,240]{1,0:T(8,128)S(1)}, f32[240,240]{1,0:T(8,128)}, u32[]{:S(2)}) copy-start(f32[240,240]{1,0:T(8,128)} %f3w_ref.1) | copy-start | bytes 691204
  16.8 2.1 %copy-start.7 = (f32[9,8,128]{2,1,0:T(8,128)S(1)}, f32[9,8,128]{2,1,0:T(8,128)}, u32[]{:S(2)}) copy-start(f32[9,8,128]{2,1,0:T(8,128)} %halo.1.ghost_ref) | copy-start | bytes 110596
  16.8 2.1 %copy-start.8 = (s32[1,1,1,128,128]{4,3,2,1,0:T(8,128)S(1)}, s32[1,1,1,128,128]{4,3,2,1,0:T(8,128)}, u32[]{:S(2)}) copy-start(s32[1,1,1,128,128]{4,3,2,1,0:T(8,128)} %param.25) | copy-start | bytes 196612
  16.8 2.1 %copy-start.11 = (f32[50,100]{1,0:T(8,128)S(1)}, f32[50,100]{1,0:T(8,128)}, u32[]{:S(2)}) copy-start(f32[50,100]{1,0:T(8,128)} %e3w_ref.1) | copy-start | bytes 60004
  16.8 2.1 %copy-start.12 = (f32[25,50]{1,0:T(8,128)S(1)}, f32[25,50]{1,0:T(8,128)}, u32[]{:S(2)}) copy-start(f32[25,50]{1,0:T(8,128)} %e2w_ref.1) | copy-start | bytes 15004
  16.8 2.1 %copy-start.14 = (f32[2,25]{1,0:T(2,128)S(1)}, f32[2,25]{1,0:T(2,128)}, u32[]{:S(2)}) copy-start(f32[2,25]{1,0:T(2,128)} %e1w_ref.1) | copy-start | bytes 604
  16.8 2.1 %copy-start.15 = (f32[2,25]{1,0:T(2,128)S(1)}, f32[2,25]{1,0:T(2,128)}, u32[]{:S(2)}) copy-start(f32[2,25]{1,0:T(2,128)} %e1b_ref.1) | copy-start | bytes 604
  16.9 2.1 %copy-start.16 = (f32[240]{0:T(256)S(1)}, f32[240]{0:T(256)}, u32[]{:S(2)}) copy-start(f32[240]{0:T(256)} %param.33) | copy-start | bytes 2884
  16.9 2.1 %copy-start.17 = (f32[240]{0:T(256)S(1)}, f32[240]{0:T(256)}, u32[]{:S(2)}) copy-start(f32[240]{0:T(256)} %param.35) | copy-start | bytes 2884
  16.9 2.1 %copy-start.18 = (f32[240]{0:T(256)S(1)}, f32[240]{0:T(256)}, u32[]{:S(2)}) copy-start(f32[240]{0:T(256)} %param.37) | copy-start | bytes 2884
  16.9 2.1 %copy-start.19 = (f32[50]{0:T(128)S(1)}, f32[50]{0:T(128)}, u32[]{:S(2)}) copy-start(f32[50]{0:T(128)} %param.29) | copy-start | bytes 604
  16.9 2.1 %copy-start.20 = (f32[100]{0:T(128)S(1)}, f32[100]{0:T(128)}, u32[]{:S(2)}) copy-start(f32[100]{0:T(128)} %param.31) | copy-start | bytes 1204
  19.0 18.5 %copy-start = (f32[2,128,768]{2,1,0:T(8,128)S(1)}, f32[2,128,768]{2,1,0:T(8,128)}, u32[]{:S(2)}) copy-start(f32[2,128,768]{2,1,0:T(8,128)} %constant.18.clone.twiddle_ref) | copy-start | bytes 2359300
  19.0 18.5 %copy-start.1 = (f32[2,128,512]{2,1,0:T(8,128)S(1)}, f32[2,128,512]{2,1,0:T(8,128)}, u32[]{:S(2)}) copy-start(f32[2,128,512]{2,1,0:T(8,128)} %constant.21.clone.green_ref) | copy-start | bytes 1572868
  19.0 18.5 %copy-start.2 = (bf16[2,256,256]{2,1,0:T(8,128)(2,1)S(1)}, bf16[2,256,256]{2,1,0:T(8,128)(2,1)}, u32[]{:S(2)}) copy-start(bf16[2,256,256]{2,1,0:T(8,128)(2,1)} %constant.17.clone.dft_b_ref) | copy-start | bytes 786436
  19.0 18.4 %copy-start.3 = (bf16[2,256,256]{2,1,0:T(8,128)(2,1)S(1)}, bf16[2,256,256]{2,1,0:T(8,128)(2,1)}, u32[]{:S(2)}) copy-start(bf16[2,256,256]{2,1,0:T(8,128)(2,1)} %constant.16.clone.dft_y_ref) | copy-start | bytes 786436
  19.1 18.4 %copy-start.6 = (f32[2,40,512]{2,1,0:T(8,128)S(1)}, f32[2,40,512]{2,1,0:T(8,128)}, u32[]{:S(2)}) copy-start(f32[2,40,512]{2,1,0:T(8,128)} %constant.19.clone.fac_x_ref) | copy-start | bytes 491524
  19.1 18.4 %copy-start.9 = (f32[2,16,512]{2,1,0:T(8,128)S(1)}, f32[2,16,512]{2,1,0:T(8,128)}, u32[]{:S(2)}) copy-start(f32[2,16,512]{2,1,0:T(8,128)} %constant.20.clone.fac_z_ref) | copy-start | bytes 196612
  19.1 18.4 %copy-start.10 = (f32[8,128]{1,0:T(8,128)S(1)}, f32[8,128]{1,0:T(8,128)}, u32[]{:S(2)}) copy-start(f32[8,128]{1,0:T(8,128)} %maximum_maximum_fusion.own_ref) | copy-start | bytes 12292
  19.1 18.4 %copy-start.13 = (f32[2,129]{1,0:T(2,128)S(1)}, f32[2,129]{1,0:T(2,128)}, u32[]{:S(2)}) copy-start(f32[2,129]{1,0:T(2,128)} %constant.22.clone.column_ref) | copy-start | bytes 3100

commit v2 on v1

--- a/solution.py
+++ b/solution.py
@@ -73,7 +73,7 @@
     return jnp.where((offset >= 0.0) & (offset < 4.0), value, 0.0)
 
 
-def halo_kernel(own_ref, ghost_ref, send_sem, recv_sem):
+def halo_kernel(positions_ref, species_ref, ghost_ref, own_ref, send_sem, recv_sem):
     wide = lax.axis_index("wide")
     narrow = lax.axis_index("narrow")
     steps = [(sx, sz) for sx in range(3) for sz in range(3) if (sx, sz) != (1, 1)]
@@ -82,6 +82,12 @@
     def device(sx, sz):
         return (lax.rem(wide + (NW + 1 - sx), NW), lax.rem(narrow + (NN + 1 - sz), NN))
 
+    own_ref[...] = jnp.concatenate(
+        [positions_ref[c, 0, 0] for c in range(3)]
+        + [species_ref[0, 0].astype(F32), jnp.zeros((4, ATOMS), F32)],
+        axis=0,
+    )
+    ghost_ref[4] = own_ref[...]
     for sx, sz in steps:
         pl.semaphore_signal(barrier, inc=1, device_id=device(sx, sz), device_id_type=MESH)
     pl.semaphore_wait(barrier, len(steps))
@@ -97,21 +103,25 @@
         )
         copy.start()
         copies.append(copy)
-    ghost_ref[4] = own_ref[...]
     for copy in copies:
         copy.wait()
 
 
-def halo(own):
+def halo(positions, species):
+    vmem = pl.BlockSpec(memory_space=pltpu.VMEM)
     return pl.pallas_call(
         halo_kernel,
         out_shape=jax.ShapeDtypeStruct((9, 8, ATOMS), F32),
-        in_specs=[pl.BlockSpec(memory_space=pltpu.VMEM)],
-        out_specs=pl.BlockSpec(memory_space=pltpu.VMEM),
-        scratch_shapes=[pltpu.SemaphoreType.DMA((8,)), pltpu.SemaphoreType.DMA((8,))],
+        in_specs=[vmem, vmem],
+        out_specs=vmem,
+        scratch_shapes=[
+            pltpu.VMEM((8, ATOMS), F32),
+            pltpu.SemaphoreType.DMA((8,)),
+            pltpu.SemaphoreType.DMA((8,)),
+        ],
         compiler_params=pltpu.CompilerParams(collective_id=0, has_side_effects=True),
         name="halo",
-    )(own)
+    )(positions, species)
 
 
 def spread_rows(rows, count):
@@ -121,7 +131,7 @@
     return jnp.where((i < 25) & (c == (r >> 5) * 25 + i), 1.0, 0.0).astype(F32)
 
 
-def net_kernel(
+def network(
     ghost_ref,
     near_ref,
     e1w_ref,
@@ -130,19 +140,17 @@
     e2b_ref,
     e3w_ref,
     e3b_ref,
+    f1b_ref,
+    f2b_ref,
+    f3b_ref,
     f1w_ref,
-    f1b_ref,
     f2w_ref,
-    f2b_ref,
     f3w_ref,
-    f3b_ref,
     fow_ref,
-    dip_ref,
     table_ref,
     own_ref,
     mat_ref,
-    left_ref,
-    right_ref,
+    arrived,
 ):
     extent = (float(CX), float(CY), float(CZ))
     for k in range(9):
@@ -222,50 +230,34 @@
             mat_ref[p, rows, :] = found[p * 8 : (p + 1) * 8]
         return carry
 
-    lax.fori_loop(0, ATOMS // 8, group, 0)
-
-    matrix = [exact(mat_ref[p], pick3) for p in range(4)]
-    left_ref[...] = f1w_ref[:, :128]
-    right_ref[...] = jnp.concatenate([f1w_ref[:, 128:], jnp.zeros((1600, 16), F32)], axis=1)
-    hidden = jnp.zeros((ATOMS, 256), F32)
-    for e in range(16):
-        entry = matrix[0] * matrix[0][:, e : e + 1]
-        for p in range(1, 4):
-            entry = entry + matrix[p] * matrix[p][:, e : e + 1]
-        weight = jnp.concatenate(
-            [left_ref[pl.ds(e, 100, stride=16), :], right_ref[pl.ds(e, 100, stride=16), :]], axis=1
-        )
-        hidden = hidden + mm3(split(entry), split(weight))
-    hidden = hidden[:, :240]
+    lax.fori_loop(0, ATOMS // 8, group, 0, unroll=4)
+
+    row = iota((ATOMS, ATOMS), 0)
+    lane = iota((ATOMS, ATOMS), 1)
+    inner = row & 31
+    kept = jnp.where(inner < 25, (row >> 5) * 25 + inner, -1)
+    pick = [jnp.where(kept == (lane >> 4) + 8 * t, 1.0, 0.0).astype(BF16) for t in range(13)]
+    pick.append(jnp.where(row == (lane & 15), 1.0, 0.0).astype(BF16))
+    pick = jnp.concatenate(pick, axis=1)
+    matrix = [mat_ref[p] for p in range(4)]
+    entries = None
+    for p in range(4):
+        high, low = split(matrix[p])
+        wide = mm(high, pick) + mm(low, pick)
+        tiled = wide[:, 1664:]
+        term = jnp.concatenate([wide[:, t * 128 : (t + 1) * 128] * tiled for t in range(13)], axis=1)
+        entries = term if entries is None else entries + term
+    arrived()
+    hidden = mm3(split(entries[:, :1600]), split(f1w_ref[...]), NT)
     hidden = jnp.tanh(hidden + f1b_ref[...])
     hidden = hidden + jnp.tanh(mm3(split(hidden), split(f2w_ref[...])) + f2b_ref[...])
     hidden = hidden + jnp.tanh(mm3(split(hidden), split(f3w_ref[...])) + f3b_ref[...])
-    coeffs = mm3(split(hidden), split(fow_ref[...]))
-    lane = iota((ATOMS, ATOMS), 1)
+    coeffs = mm3(split(hidden), split(exact(pick3, fow_ref[...])), NT)
     result = jnp.zeros((ATOMS, ATOMS), F32)
     for c in range(3):
         total = jnp.sum(coeffs * matrix[1 + c], axis=1, keepdims=True)
         result = jnp.where(lane == c, total, result)
-    dip_ref[...] = result.T[:8]
-
-
-def net(ghosts, neighbours, weights):
-    vmem = pl.BlockSpec(memory_space=pltpu.VMEM)
-    return pl.pallas_call(
-        net_kernel,
-        out_shape=jax.ShapeDtypeStruct((8, ATOMS), F32),
-        in_specs=[vmem] * (2 + len(weights)),
-        out_specs=vmem,
-        scratch_shapes=[
-            pltpu.VMEM((36, 8, ATOMS), F32),
-            pltpu.VMEM((3, ATOMS, ATOMS), F32),
-            pltpu.VMEM((4, ATOMS, ATOMS), F32),
-            pltpu.VMEM((1600, ATOMS), F32),
-            pltpu.VMEM((1600, ATOMS), F32),
-        ],
-        compiler_params=pltpu.CompilerParams(vmem_limit_bytes=32 << 20),
-        name="net",
-    )(ghosts, neighbours, *weights)
+    return result.T[:8]
 
 
 def np_split(x):
@@ -317,30 +309,72 @@
     return dft_y, dft_b, twiddle, fac_x, fac_z, green, column
 
 
-def long_kernel(
-    own_ref,
-    dip_ref,
-    dft_y_ref,
-    dft_b_ref,
-    twiddle_ref,
-    fac_x_ref,
-    fac_z_ref,
-    green_ref,
-    column_ref,
-    dipole_ref,
-    atom_ref,
-    centroid_ref,
-    energy_ref,
-    mix_ref,
-    wave_ref,
-    tab_ref,
-    out_one,
-    in_one,
-    out_two,
-    in_two,
-    send_sem,
-    recv_sem,
-):
+EARLY = (
+    ((9, 8, ATOMS), F32),
+    ((ATOMS, ATOMS), jnp.int32),
+    ((2, 25), F32),
+    ((2, 25), F32),
+    ((25, 50), F32),
+    ((1, 50), F32),
+    ((50, 100), F32),
+    ((1, 100), F32),
+    ((1, 240), F32),
+    ((1, 240), F32),
+    ((1, 240), F32),
+)
+LATE = (
+    ((240, 1600), F32),
+    ((240, 240), F32),
+    ((240, 240), F32),
+    ((100, 240), F32),
+    ((2, 256, CY), BF16),
+    ((2, 256, 256), BF16),
+    ((2, ND, TILE), F32),
+    ((2, TX, MODES), F32),
+    ((2, 16, MODES), F32),
+    ((2, ND, MODES), F32),
+)
+
+
+def main_kernel(*refs):
+    count = len(EARLY) + len(LATE)
+    column_ref = refs[0]
+    far = refs[1 : 1 + count]
+    result_ref = refs[1 + count]
+    near = refs[2 + count : 2 + 2 * count]
+    (
+        ghost_ref,
+        near_ref,
+        e1w_ref,
+        e1b_ref,
+        e2w_ref,
+        e2b_ref,
+        e3w_ref,
+        e3b_ref,
+        f1b_ref,
+        f2b_ref,
+        f3b_ref,
+    ) = near[: len(EARLY)]
+    (
+        table_ref,
+        home_ref,
+        mat_ref,
+        mix_ref,
+        wave_ref,
+        tab_ref,
+        out_one,
+        in_one,
+        out_two,
+        in_two,
+        late_sem,
+        send_sem,
+        recv_sem,
+    ) = refs[2 + 2 * count :]
+    f1w_ref, f2w_ref, f3w_ref, fow_ref = near[len(EARLY) : len(EARLY) + 4]
+    dft_y_ref, dft_b_ref, twiddle_ref, fac_x_ref, fac_z_ref, green_ref = near[len(EARLY) + 4 :]
+    fetch = [pltpu.make_async_copy(far[i], near[i], late_sem.at[i]) for i in range(count)]
+    for copy in fetch:
+        copy.start()
     wide = lax.axis_index("wide")
     narrow = lax.axis_index("narrow")
     me = wide * NN + narrow
@@ -356,14 +390,41 @@
 
     lax.fori_loop(1, ND, greet, 0)
 
-    kind = own_ref[3:4, :]
+    def arrived():
+        for copy in fetch[len(EARLY) :]:
+            copy.wait()
+
+    for copy in fetch[: len(EARLY)]:
+        copy.wait()
+    dip = network(
+        ghost_ref,
+        near_ref,
+        e1w_ref,
+        e1b_ref,
+        e2w_ref,
+        e2b_ref,
+        e3w_ref,
+        e3b_ref,
+        f1b_ref,
+        f2b_ref,
+        f3b_ref,
+        f1w_ref,
+        f2w_ref,
+        f3w_ref,
+        fow_ref,
+        table_ref,
+        home_ref,
+        mat_ref,
+        arrived,
+    )
+
+    kind = ghost_ref[4, 3:4, :]
     oxygen = 1.0 - kind
-    dip = dip_ref[...]
-    dipole_ref[...] = dip * oxygen
+    result_ref[0:8, :] = dip * oxygen
     shift = 0.5 * jnp.tanh(dip)
 
     def sites(c, extent):
-        atom = own_ref[c : c + 1, :] * float(extent)
+        atom = ghost_ref[4, c : c + 1, :] * float(extent)
         return jnp.concatenate([atom, atom + shift[c : c + 1, :]], axis=1)
 
     charge = jnp.concatenate([6.0 * oxygen + kind, -8.0 * oxygen], axis=1)
@@ -521,29 +582,56 @@
         -jnp.sum(wave_slope * inner[:, :256], axis=0, keepdims=True),
         -jnp.sum(wave * inner[:, 512:], axis=0, keepdims=True),
     ]
+    total = jnp.sum(planes[:128, TILE - 1 : TILE], axis=0, keepdims=True)
+    atom = [r[:, :128] for r in rows]
+    centroid = [r[:, 128:] * oxygen for r in rows]
+    result_ref[8:24, :] = jnp.concatenate(
+        atom + centroid + [jnp.broadcast_to(total, (8, ATOMS))], axis=0
+    )
+
+
+def deal_kernel(result_ref, dipole_ref, atom_ref, centroid_ref, energy_ref):
+    for c in range(3):
+        dipole_ref[c, 0, 0] = result_ref[c : c + 1, :]
     for c in range(4):
-        atom_ref[c : c + 1, :] = rows[c][:, :128]
-        centroid_ref[c : c + 1, :] = rows[c][:, 128:] * oxygen
-    energy_ref[...] = jnp.broadcast_to(
-        jnp.sum(planes[:128, TILE - 1 : TILE], axis=0, keepdims=True), (8, 128)
-    )
-
-
-def long_range(own, dip):
+        atom_ref[c, 0, 0] = result_ref[8 + c : 9 + c, :]
+        centroid_ref[c, 0, 0] = result_ref[12 + c : 13 + c, :]
+    energy_ref[...] = result_ref[16:17, 0:1]
+
+
+def local(
+    positions,
+    species,
+    neighbours,
+    e1w,
+    e1b,
+    e2w,
+    e2b,
+    e3w,
+    e3b,
+    f1w,
+    f1b,
+    f2w,
+    f2b,
+    f3w,
+    f3b,
+    fow,
+):
+    ghosts = halo(positions, species)
+    *late, column = [jnp.asarray(t) for t in tables()]
     vmem = pl.BlockSpec(memory_space=pltpu.VMEM)
-    smem = pl.BlockSpec(memory_space=pltpu.SMEM)
-    consts = [jnp.asarray(t) for t in tables()]
-    return pl.pallas_call(
-        long_kernel,
-        out_shape=(
-            jax.ShapeDtypeStruct((8, ATOMS), F32),
-            jax.ShapeDtypeStruct((4, ATOMS), F32),
-            jax.ShapeDtypeStruct((4, ATOMS), F32),
-            jax.ShapeDtypeStruct((8, ATOMS), F32),
-        ),
-        in_specs=[vmem] * 8 + [smem],
-        out_specs=(vmem,) * 4,
-        scratch_shapes=[
+    anywhere = pl.BlockSpec(memory_space=pl.ANY)
+    row = lambda x: x.reshape(1, -1)
+    result = pl.pallas_call(
+        main_kernel,
+        out_shape=jax.ShapeDtypeStruct((24, ATOMS), F32),
+        in_specs=[pl.BlockSpec(memory_space=pltpu.SMEM)] + [anywhere] * (len(EARLY) + len(LATE)),
+        out_specs=vmem,
+        scratch_shapes=[pltpu.VMEM(shape, dtype) for shape, dtype in EARLY + LATE]
+        + [
+            pltpu.VMEM((36, 8, ATOMS), F32),
+            pltpu.VMEM((3, ATOMS, ATOMS), F32),
+            pltpu.VMEM((4, ATOMS, ATOMS), F32),
             pltpu.VMEM((2, TILE, TILE), BF16),
             pltpu.VMEM((CY, 512), F32),
             pltpu.VMEM((2, FOLD, MODES), F32),
@@ -551,35 +639,46 @@
             pltpu.VMEM((ND, 12, 128), F32),
             pltpu.VMEM((ND, 12, 128), F32),
             pltpu.VMEM((ND, 12, 128), F32),
+            pltpu.SemaphoreType.DMA((len(EARLY) + len(LATE),)),
             pltpu.SemaphoreType.DMA((2,)),
             pltpu.SemaphoreType.DMA((2,)),
         ],
         compiler_params=pltpu.CompilerParams(
-            collective_id=1, has_side_effects=True, vmem_limit_bytes=50 << 20
+            collective_id=1, has_side_effects=True, vmem_limit_bytes=58 << 20
         ),
-        name="long_range",
-    )(own, dip, *consts)
-
-
-def local(positions, species, neighbours, *weights):
-    own = jnp.concatenate(
-        [
-            positions.reshape(3, ATOMS),
-            species.reshape(1, ATOMS).astype(F32),
-            jnp.zeros((4, ATOMS), F32),
-        ],
-        axis=0,
-    )
-    ghosts = halo(own)
-    weights = [w.reshape(1, -1) if w.ndim == 1 else w for w in weights]
-    dip = net(ghosts, neighbours.reshape(ATOMS, ATOMS), weights)
-    dipole, atom, centroid, energy = long_range(own, dip)
-    return (
-        dipole[:3].reshape(3, 1, 1, 1, ATOMS),
-        atom.reshape(4, 1, 1, 1, ATOMS),
-        centroid.reshape(4, 1, 1, 1, ATOMS),
-        energy[0, 0],
-    )
+        name="main",
+    )(
+        column,
+        ghosts,
+        neighbours.reshape(ATOMS, ATOMS),
+        e1w,
+        e1b,
+        e2w,
+        row(e2b),
+        e3w,
+        row(e3b),
+        row(f1b),
+        row(f2b),
+        row(f3b),
+        f1w.T,
+        f2w,
+        f3w,
+        fow.T,
+        *late,
+    )
+    dipole, atom, centroid, energy = pl.pallas_call(
+        deal_kernel,
+        out_shape=(
+            jax.ShapeDtypeStruct((3, 1, 1, 1, ATOMS), F32),
+            jax.ShapeDtypeStruct((4, 1, 1, 1, ATOMS), F32),
+            jax.ShapeDtypeStruct((4, 1, 1, 1, ATOMS), F32),
+            jax.ShapeDtypeStruct((1, 1), F32),
+        ),
+        in_specs=[vmem],
+        out_specs=(vmem,) * 4,
+        name="deal",
+    )(result)
+    return dipole, atom, centroid, energy.reshape(())
 
 
 def solution(mesh):

time: 85.8 us -> 71.8 us (0.84)
  Pallas kernels: 77.2 us -> 70.9 us
  local copies, waits for them, and re-layouts: 6.07 us -> 0 us
  other arithmetic: 1.31 us -> 0 us
    pallas_call x2, Pallas kernels: 64.1 us -> 57.7 us  [the longest x1 56.4 us: local(): pl.pallas_call(main_kernel, out_shape=jax.ShapeDtypeStruct((24, ATOMS), F...]
    unnamed x48 -> x0, local copies, waits for them, and re-layouts: 5.47 us -> none
where the time goes in v2:
time: 71.8 us; the launch traced here: 71.5 us
  Pallas kernels  70.9 us (99%)
    pallas_call x1, Pallas kernels, local(): pl.pallas_call(main_kernel, out_shape=jax.ShapeDtypeStruct((24, ATOMS), F...  56.4 us
    pallas_call x1, Pallas kernels, halo(): pl.pallas_call(halo_kernel, out_shape=jax.ShapeDtypeStruct((9, 8, ATOMS),...  13.2 us

profile of v2, /device:TPU:1, one launch (start us, length us, event | category | flops | bytes accessed | tf_op | source)
XLA Modules:
  0.0 71.5 jit_solution(14002120749852165464)
XLA Ops:
  0.6 13.2 %halo.1.refs_1_ = f32[9,8,128]{2,1,0:T(8,128)} custom-call(f32[3,1,1,1,128]{4,3,2,1,0:T(1,128)} %positions_ref.1, s32[1,1,1,128]{3,2,1,0:T(1,128)} %species_ref.1), custom_call_target="tpu_custom_call" | custom-call | tf_op jit(solution)/shard_map/halo/pallas_call | solution.py:112
  13.8 56.4 %main.1.result_ref = f32[24,128]{1,0:T(8,128)} custom-call(f32[2,129]{1,0:T(2,128)} %constant.20.clone.refs_0_, f32[9,8,128]{2,1,0:T(8,128)} %halo.1.refs_1_, s32[128,128]{1,0:T(8,128)} %bitcast.11, f32[2,25]{1,0:T(2,128)} %refs_3_.1, f32[2,25]{1,0:T(2,128)} %refs_4_.1, f32[25,50]{1,0:T(8,128)} %refs_5_.1, f32[1,50]{1,0:T(1,128)} %bitcast.15, ...), custom_call_target="tpu_custom_call" | custom-call | tf_op jit(solution)/shard_map/main/pallas_call | solution.py:625
  70.2 1.3 %deal.1 = (f32[3,1,1,1,128]{4,3,2,1,0:T(1,128)}, f32[4,1,1,1,128]{4,3,2,1,0:T(1,128)}, f32[4,1,1,1,128]{4,3,2,1,0:T(1,128)}, f32[1,1]{1,0:T(1,128)}) custom-call(f32[24,128]{1,0:T(8,128)} %main.1.result_ref), custom_call_target="tpu_custom_call" | custom-call | tf_op jit(solution)/shard_map/deal/pallas_call | solution.py:669

commit v3 on v2

--- a/solution.py
+++ b/solution.py
@@ -12,9 +12,10 @@
 NW, NN = 8, 16
 ND = NW * NN
 CX, CY, CZ = 32, 256, 16
-TX, TZ = 40, 19
-TILE = 768
-FOLD = 640
+TX, TZ = 32, 19
+TILE = 640
+FOLD = 512
+ROWS = 10
 MODES = 512
 ATOMS = 128
 F32 = jnp.float32
@@ -280,10 +281,10 @@
     cos, sin = np.cos(phi), np.sin(phi)
     dft_b = np_split(np.block([[cos, sin], [-sin, cos]]))
     z, x = np.divmod(np.arange(TILE), TX)
-    turn = 2 * np.pi * ((j[:, None] * (x - 3)[None] + k[:, None] * (z - 3)[None]) % 256) / 256
+    turn = 2 * np.pi * ((j[:, None] * (x - 1)[None] + k[:, None] * (z - 3)[None]) % 256) / 256
     twiddle = np.stack([np.cos(turn), np.sin(turn)]).astype(np.float32)
     v, u = np.divmod(np.arange(MODES), 32)
-    ax = 2 * np.pi * ((np.arange(TX)[:, None] - 3) * u[None] % 32) / 32
+    ax = 2 * np.pi * ((np.arange(TX)[:, None] - 1) * u[None] % 32) / 32
     az = 2 * np.pi * ((np.arange(16)[:, None] - 3) * v[None] % 16) / 16
     fac_x = np.stack([np.cos(ax), np.sin(ax)]).astype(np.float32)
     fac_z = np.stack([np.cos(az), np.sin(az)]).astype(np.float32)
@@ -428,7 +429,7 @@
         return jnp.concatenate([atom, atom + shift[c : c + 1, :]], axis=1)
 
     charge = jnp.concatenate([6.0 * oxygen + kind, -8.0 * oxygen], axis=1)
-    off_x = sites(0, CX) - (iota((TX, 256), 0).astype(F32) - 3.0)
+    off_x = sites(0, CX) - (iota((TX, 256), 0).astype(F32) - 1.0)
     off_z = sites(2, CZ) - (iota((24, 256), 0).astype(F32) - 3.0)
     off_y = sites(1, CY) - iota((CY, 256), 0).astype(F32)
     off_y = jnp.where(off_y < 0.0, off_y + float(CY), off_y)
@@ -449,8 +450,8 @@
         split(wave[:, :256] * charge), (mix_ref[0, :, :256], mix_ref[1, :, :256]), NT
     )
     for part in range(2):
-        for t in range(6):
-            out_one[:, part * 6 + t, :] = spread[part * 128 : (part + 1) * 128, t * 128 : (t + 1) * 128]
+        for t in range(5):
+            out_one[:, part * 5 + t, :] = spread[part * 128 : (part + 1) * 128, t * 128 : (t + 1) * 128]
 
     pl.semaphore_wait(barrier, ND - 1)
 
@@ -502,7 +503,7 @@
     def gathered(in_ref):
         return jnp.concatenate(
             [
-                jnp.concatenate([in_ref[:, part * 6 + t, :] for t in range(6)], axis=1)
+                jnp.concatenate([in_ref[:, part * 5 + t, :] for t in range(5)], axis=1)
                 for part in range(2)
             ],
             axis=0,
@@ -562,27 +563,78 @@
     partial = jnp.sum(tiles[:128] * field_r + tiles[128:] * field_i, keepdims=True)
     partial = partial * (0.5 / (ND * ATOMS))
     lane = iota((ND, 128), 1)
-    for t in range(6):
+    for t in range(5):
         piece = field_r[:, t * 128 : (t + 1) * 128]
-        if t == 5:
+        if t == 4:
             piece = jnp.where(lane == 127, partial, piece)
         out_two[:, t, :] = piece
-        out_two[:, 6 + t, :] = field_i[:, t * 128 : (t + 1) * 128]
-
-    exchange(out_two, in_two, 1)
-    settle(out_two, in_two, 1)
-
-    planes = gathered(in_two)
-    inner = mm3(split(planes), (mix_ref[0], mix_ref[1]))
-    wave = wave_ref[:, :256]
-    wave_slope = wave_ref[:, 256:]
-    rows = [
-        jnp.sum(wave * inner[:, :256], axis=0, keepdims=True),
-        -jnp.sum(wave * inner[:, 256:512], axis=0, keepdims=True),
-        -jnp.sum(wave_slope * inner[:, :256], axis=0, keepdims=True),
-        -jnp.sum(wave * inner[:, 512:], axis=0, keepdims=True),
-    ]
-    total = jnp.sum(planes[:128, TILE - 1 : TILE], axis=0, keepdims=True)
+        out_two[:, 5 + t, :] = field_i[:, t * 128 : (t + 1) * 128]
+
+    def place(c, i):
+        step = c * 2 + i // NN
+        w = lax.rem(wide + step, NW)
+        n = lax.rem(narrow + lax.rem(i, NN), NN)
+        return w * NN + n, (w, n)
+
+    for c in range(4):
+
+        def one(i, carry):
+            at, device = place(c, i)
+            pltpu.make_async_remote_copy(
+                src_ref=out_two.at[at],
+                dst_ref=in_two.at[me],
+                send_sem=send_sem.at[1],
+                recv_sem=recv_sem.at[1 + c],
+                device_id=device,
+                device_id_type=MESH,
+            ).start()
+            return carry
+
+        lax.fori_loop(1 if c == 0 else 0, 32, one, 0)
+    in_two[me] = out_two[me]
+    mix = (mix_ref[0], mix_ref[1])
+    rows = [jnp.zeros((1, 256), F32)] * 4
+    total = jnp.zeros((1, 1), F32)
+    for c in range(4):
+        size = 31 if c == 0 else 32
+        pltpu.make_async_remote_copy(
+            src_ref=out_two.at[pl.ds(0, size)],
+            dst_ref=in_two.at[pl.ds(0, size)],
+            send_sem=send_sem.at[1],
+            recv_sem=recv_sem.at[1 + c],
+            device_id=peer(1)[1],
+            device_id_type=MESH,
+        ).wait_recv()
+        spans = [lax.rem(wide + (NW - 2 * c - i), NW) * NN for i in range(2)]
+        spans = [pl.ds(pl.multiple_of(at, NN), NN) for at in spans]
+        lower = [pl.ds(pl.multiple_of(at.start + ND, NN), NN) for at in spans]
+        planes = jnp.concatenate(
+            [
+                jnp.concatenate([in_two[at, part * 5 + t, :] for t in range(5)], axis=1)
+                for part in range(2)
+                for at in spans
+            ],
+            axis=0,
+        )
+        inner = mm3(split(planes), mix)
+        wave = jnp.concatenate([wave_ref[at, :] for at in spans + lower], axis=0)
+        wave, wave_slope = wave[:, :256], wave[:, 256:]
+        parts = [
+            wave * inner[:, :256],
+            -wave * inner[:, 256:512],
+            -wave_slope * inner[:, :256],
+            -wave * inner[:, 512:],
+        ]
+        rows = [r + jnp.sum(p, axis=0, keepdims=True) for r, p in zip(rows, parts)]
+        total = total + jnp.sum(planes[:32, TILE - 1 : TILE], axis=0, keepdims=True)
+    pltpu.make_async_remote_copy(
+        src_ref=out_two.at[pl.ds(0, ND - 1)],
+        dst_ref=in_two.at[pl.ds(0, ND - 1)],
+        send_sem=send_sem.at[1],
+        recv_sem=recv_sem.at[1],
+        device_id=peer(1)[1],
+        device_id_type=MESH,
+    ).wait_send()
     atom = [r[:, :128] for r in rows]
     centroid = [r[:, 128:] * oxygen for r in rows]
     result_ref[8:24, :] = jnp.concatenate(
@@ -632,16 +684,16 @@
             pltpu.VMEM((36, 8, ATOMS), F32),
             pltpu.VMEM((3, ATOMS, ATOMS), F32),
             pltpu.VMEM((4, ATOMS, ATOMS), F32),
-            pltpu.VMEM((2, TILE, TILE), BF16),
+            pltpu.VMEM((2, TILE, 768), BF16),
             pltpu.VMEM((CY, 512), F32),
             pltpu.VMEM((2, FOLD, MODES), F32),
-            pltpu.VMEM((ND, 12, 128), F32),
-            pltpu.VMEM((ND, 12, 128), F32),
-            pltpu.VMEM((ND, 12, 128), F32),
-            pltpu.VMEM((ND, 12, 128), F32),
+            pltpu.VMEM((ND, ROWS, 128), F32),
+            pltpu.VMEM((ND, ROWS, 128), F32),
+            pltpu.VMEM((ND, ROWS, 128), F32),
+            pltpu.VMEM((ND, ROWS, 128), F32),
             pltpu.SemaphoreType.DMA((len(EARLY) + len(LATE),)),
             pltpu.SemaphoreType.DMA((2,)),
-            pltpu.SemaphoreType.DMA((2,)),
+            pltpu.SemaphoreType.DMA((5,)),
         ],
         compiler_params=pltpu.CompilerParams(
             collective_id=1, has_side_effects=True, vmem_limit_bytes=58 << 20

time: 71.8 us -> 66.5 us (0.926)
  Pallas kernels: 70.9 us -> 65.6 us
    pallas_call x1, Pallas kernels: 56.4 us -> 51.1 us  [local(): pl.pallas_call(main_kernel, out_shape=jax.ShapeDtypeStruct((24, ATOMS), F...]
where the time goes in v3:
time: 66.5 us; the launch traced here: 66.2 us
  Pallas kernels  65.6 us (99%)
    pallas_call x1, Pallas kernels, local(): pl.pallas_call(main_kernel, out_shape=jax.ShapeDtypeStruct((24, ATOMS), F...  51.1 us
    pallas_call x1, Pallas kernels, halo(): pl.pallas_call(halo_kernel, out_shape=jax.ShapeDtypeStruct((9, 8, ATOMS),...  13.2 us

profile of v3, /device:TPU:1, one launch (start us, length us, event | category | flops | bytes accessed | tf_op | source)
XLA Modules:
  0.0 66.2 jit_solution(10349743544320929022)
XLA Ops:
  0.6 13.2 %halo.1.refs_1_ = f32[9,8,128]{2,1,0:T(8,128)} custom-call(f32[3,1,1,1,128]{4,3,2,1,0:T(1,128)} %positions_ref.1, s32[1,1,1,128]{3,2,1,0:T(1,128)} %species_ref.1), custom_call_target="tpu_custom_call" | custom-call | tf_op jit(solution)/shard_map/halo/pallas_call | solution.py:113
  13.8 51.1 %main.1.result_ref = f32[24,128]{1,0:T(8,128)} custom-call(f32[2,129]{1,0:T(2,128)} %constant.20.clone.refs_0_, f32[9,8,128]{2,1,0:T(8,128)} %halo.1.refs_1_, s32[128,128]{1,0:T(8,128)} %bitcast.11, f32[2,25]{1,0:T(2,128)} %refs_3_.1, f32[2,25]{1,0:T(2,128)} %refs_4_.1, f32[25,50]{1,0:T(8,128)} %refs_5_.1, f32[1,50]{1,0:T(1,128)} %bitcast.15, ...), custom_call_target="tpu_custom_call" | custom-call | tf_op jit(solution)/shard_map/main/pallas_call | solution.py:677
  64.9 1.3 %deal.1 = (f32[3,1,1,1,128]{4,3,2,1,0:T(1,128)}, f32[4,1,1,1,128]{4,3,2,1,0:T(1,128)}, f32[4,1,1,1,128]{4,3,2,1,0:T(1,128)}, f32[1,1]{1,0:T(1,128)}) custom-call(f32[24,128]{1,0:T(8,128)} %main.1.result_ref), custom_call_target="tpu_custom_call" | custom-call | tf_op jit(solution)/shard_map/deal/pallas_call | solution.py:721

commit v4 on v3

--- a/solution.py
+++ b/solution.py
@@ -16,6 +16,7 @@
 TILE = 640
 FOLD = 512
 ROWS = 10
+WIDTH = 8
 MODES = 512
 ATOMS = 128
 F32 = jnp.float32
@@ -48,30 +49,14 @@
 
 
 def spline(offset):
-    square = offset * offset
-    cube = square * offset
-    remain = 4.0 - offset
-    one = cube * (1.0 / 6.0)
-    two = (-3.0 * cube + 12.0 * square - 12.0 * offset + 4.0) * (1.0 / 6.0)
-    three = (3.0 * cube - 24.0 * square + 60.0 * offset - 44.0) * (1.0 / 6.0)
-    four = remain * remain * remain * (1.0 / 6.0)
-    value = jnp.where(
-        offset < 1.0, one, jnp.where(offset < 2.0, two, jnp.where(offset < 3.0, three, four))
-    )
-    return jnp.where((offset >= 0.0) & (offset < 4.0), value, 0.0)
-
-
-def slope(offset):
-    square = offset * offset
-    remain = 4.0 - offset
-    one = square * 0.5
-    two = (-9.0 * square + 24.0 * offset - 12.0) * (1.0 / 6.0)
-    three = (9.0 * square - 48.0 * offset + 60.0) * (1.0 / 6.0)
-    four = -0.5 * remain * remain
-    value = jnp.where(
-        offset < 1.0, one, jnp.where(offset < 2.0, two, jnp.where(offset < 3.0, three, four))
-    )
-    return jnp.where((offset >= 0.0) & (offset < 4.0), value, 0.0)
+    from_middle = offset - 2.0
+    away = jnp.abs(from_middle)
+    outer = jnp.maximum(2.0 - away, 0.0)
+    inner = jnp.maximum(1.0 - away, 0.0)
+    outer_square, inner_square = outer * outer, inner * inner
+    value = (outer_square * outer - 4.0 * (inner_square * inner)) * (1.0 / 6.0)
+    fall = 0.5 * outer_square - 2.0 * inner_square
+    return value, jnp.where(from_middle > 0.0, -fall, fall)
 
 
 def halo_kernel(positions_ref, species_ref, ghost_ref, own_ref, send_sem, recv_sem):
@@ -177,12 +162,15 @@
     bias3 = column(pick3, e3b_ref[...])
     w2 = exact(pick2, exact(pick1, e2w_ref[...]), NT)
     w3 = exact(pick3, exact(pick2, e3w_ref[...]), NT)
+    last = iota((32, ATOMS), 0) == 31
+    b_oxygen = jnp.where(last, 20.0, b_oxygen)
+    b_hydrogen = jnp.where(last, 20.0, b_hydrogen)
+    w2 = jnp.where(iota((64, 32), 1) == 31, bias2[:, :32], w2)
+    w3 = jnp.where(iota((128, 64), 1) == 31, bias3[:, :64], w3)
     w2_high, w2_low = split(w2)
     w3_high, w3_low = split(w3)
     w2_all = jnp.concatenate([w2_high, w2_high, w2_low], axis=1)
     w3_all = jnp.concatenate([w3_high, w3_high, w3_low], axis=1)
-    bias2 = jnp.concatenate([bias2] * 8, axis=1)
-    bias3 = jnp.concatenate([bias3] * 8, axis=1)
     sublane = iota((8, ATOMS), 0)
 
     def group(g, carry):
@@ -203,50 +191,48 @@
         square = scaled[0] * scaled[0] + scaled[1] * scaled[1] + scaled[2] * scaled[2]
         smooth = 1.0 / (1.0 + square)
         kind = parts[3]
-        pieces = []
-        for b in range(8):
-            s = jnp.broadcast_to(smooth[b : b + 1, :], (32, ATOMS))
-            h = jnp.broadcast_to(kind[b : b + 1, :], (32, ATOMS)) > 0.5
-            pieces.append(
-                jnp.where(h, w_hydrogen, w_oxygen) * s + jnp.where(h, b_hydrogen, b_oxygen)
-            )
-        one = jnp.tanh(jnp.concatenate(pieces, axis=1))
-        high, low = split(one)
-        two = jnp.tanh(mm(w2_all, jnp.concatenate([high, low, high], axis=0)) + bias2)
-        two = two + jnp.concatenate([one, one], axis=0)
-        high, low = split(two)
-        three = jnp.tanh(mm(w3_all, jnp.concatenate([high, low, high], axis=0)) + bias3)
-        three = three + jnp.concatenate([two, two], axis=0)
-        high, low = split(three)
         scale = smooth * (1.0 / 128.0)
         radial = [scale] + [scale * scaled[c] for c in range(3)]
-        blocks = []
-        for b in range(8):
-            mine = sublane == b
-            blocks.append(jnp.concatenate([jnp.where(mine, r, 0.0) for r in radial], axis=0))
-        radial = jnp.concatenate(blocks, axis=1)
-        r_high, r_low = split(radial)
-        found = mm(r_high, high, NT) + mm(r_high, low, NT) + mm(r_low, high, NT)
+        found = jnp.zeros((32, ATOMS), F32)
+        for pair in range(8 // WIDTH):
+            pieces, blocks = [], []
+            for b in range(WIDTH * pair, WIDTH * pair + WIDTH):
+                s = jnp.broadcast_to(smooth[b : b + 1, :], (32, ATOMS))
+                h = jnp.broadcast_to(kind[b : b + 1, :], (32, ATOMS)) > 0.5
+                pieces.append(
+                    jnp.where(h, w_hydrogen, w_oxygen) * s + jnp.where(h, b_hydrogen, b_oxygen)
+                )
+                blocks.append(
+                    jnp.concatenate([jnp.where(sublane == b, r, 0.0) for r in radial], axis=0)
+                )
+            one = jnp.tanh(jnp.concatenate(pieces, axis=1))
+            high, low = split(one)
+            two = jnp.tanh(mm(w2_all, jnp.concatenate([high, low, high], axis=0)))
+            two = two + jnp.concatenate([one, one], axis=0)
+            high, low = split(two)
+            three = jnp.tanh(mm(w3_all, jnp.concatenate([high, low, high], axis=0)))
+            three = three + jnp.concatenate([two, two], axis=0)
+            high, low = split(three)
+            r_high, r_low = split(jnp.concatenate(blocks, axis=1))
+            both = mm(jnp.concatenate([r_high, r_low], axis=0), high, NT)
+            found = found + (both[:32] + both[32:]) + mm(r_high, low, NT)
         for p in range(4):
             mat_ref[p, rows, :] = found[p * 8 : (p + 1) * 8]
         return carry
 
     lax.fori_loop(0, ATOMS // 8, group, 0, unroll=4)
 
-    row = iota((ATOMS, ATOMS), 0)
     lane = iota((ATOMS, ATOMS), 1)
-    inner = row & 31
-    kept = jnp.where(inner < 25, (row >> 5) * 25 + inner, -1)
-    pick = [jnp.where(kept == (lane >> 4) + 8 * t, 1.0, 0.0).astype(BF16) for t in range(13)]
-    pick.append(jnp.where(row == (lane & 15), 1.0, 0.0).astype(BF16))
-    pick = jnp.concatenate(pick, axis=1)
+    entries = None
     matrix = [mat_ref[p] for p in range(4)]
-    entries = None
     for p in range(4):
-        high, low = split(matrix[p])
-        wide = mm(high, pick) + mm(low, pick)
-        tiled = wide[:, 1664:]
-        term = jnp.concatenate([wide[:, t * 128 : (t + 1) * 128] * tiled for t in range(13)], axis=1)
+        tiled = jnp.take_along_axis(matrix[p], lane & 15, axis=1)
+        term = []
+        for t in range(13):
+            d = jnp.minimum((lane >> 4) + 8 * t, 99)
+            block = (d * 41) >> 10
+            term.append(jnp.take_along_axis(matrix[p], d + 7 * block, axis=1) * tiled)
+        term = jnp.concatenate(term, axis=1)
         entries = term if entries is None else entries + term
     arrived()
     hidden = mm3(split(entries[:, :1600]), split(f1w_ref[...]), NT)
@@ -432,12 +418,11 @@
     off_x = sites(0, CX) - (iota((TX, 256), 0).astype(F32) - 1.0)
     off_z = sites(2, CZ) - (iota((24, 256), 0).astype(F32) - 3.0)
     off_y = sites(1, CY) - iota((CY, 256), 0).astype(F32)
-    off_y = jnp.where(off_y < 0.0, off_y + float(CY), off_y)
-    wx, sx = spline(off_x), slope(off_x)
-    wz, sz = spline(off_z), slope(off_z)
+    wx, sx = spline(off_x)
+    wz, sz = spline(off_z)
     wave = mm3(
         (dft_y_ref[0], dft_y_ref[1]),
-        split(jnp.concatenate([spline(off_y), slope(off_y)], axis=1)),
+        split(jnp.concatenate(spline(off_y), axis=1)),
     )
     wave_ref[...] = wave
     rest = jnp.zeros((TILE - TX * TZ, 256), F32)

time: 66.5 us -> 64.9 us (0.976)
  Pallas kernels: 65.6 us -> 64 us
    pallas_call x1, Pallas kernels: 51.1 us -> 49.6 us  [local(): pl.pallas_call(main_kernel, out_shape=jax.ShapeDtypeStruct((24, ATOMS), F...]
where the time goes in v4:
time: 64.9 us; the launch traced here: 64.7 us
  Pallas kernels  64 us (99%)
  between operations  0.65 us (1%)
    pallas_call x1, Pallas kernels, local(): pl.pallas_call(main_kernel, out_shape=jax.ShapeDtypeStruct((24, ATOMS), F...  49.6 us
    pallas_call x1, Pallas kernels, halo(): pl.pallas_call(halo_kernel, out_shape=jax.ShapeDtypeStruct((9, 8, ATOMS),...  13.2 us
    pallas_call x1, Pallas kernels, local(): pl.pallas_call(deal_kernel, out_shape=(jax.ShapeDtypeStruct((3, 1, 1, 1,...  1.3 us

profile of v4, /device:TPU:1, one launch (start us, length us, event | category | flops | bytes accessed | tf_op | source)
XLA Modules:
  0.0 64.7 jit_solution(7310012780610247782)
XLA Ops:
  0.6 13.2 %halo.1.refs_1_ = f32[9,8,128]{2,1,0:T(8,128)} custom-call(f32[3,1,1,1,128]{4,3,2,1,0:T(1,128)} %positions_ref.1, s32[1,1,1,128]{3,2,1,0:T(1,128)} %species_ref.1), custom_call_target="tpu_custom_call" | custom-call | tf_op jit(solution)/shard_map/halo/pallas_call | solution.py:98
  13.8 49.6 %main.1.result_ref = f32[24,128]{1,0:T(8,128)} custom-call(f32[2,129]{1,0:T(2,128)} %constant.20.clone.refs_0_, f32[9,8,128]{2,1,0:T(8,128)} %halo.1.refs_1_, s32[128,128]{1,0:T(8,128)} %bitcast.11, f32[2,25]{1,0:T(2,128)} %refs_3_.1, f32[2,25]{1,0:T(2,128)} %refs_4_.1, f32[25,50]{1,0:T(8,128)} %refs_5_.1, f32[1,50]{1,0:T(1,128)} %bitcast.15, ...), custom_call_target="tpu_custom_call" | custom-call | tf_op jit(solution)/shard_map/main/pallas_call | solution.py:662
  63.4 1.3 %deal.1 = (f32[3,1,1,1,128]{4,3,2,1,0:T(1,128)}, f32[4,1,1,1,128]{4,3,2,1,0:T(1,128)}, f32[4,1,1,1,128]{4,3,2,1,0:T(1,128)}, f32[1,1]{1,0:T(1,128)}) custom-call(f32[24,128]{1,0:T(8,128)} %main.1.result_ref), custom_call_target="tpu_custom_call" | custom-call | tf_op jit(solution)/shard_map/deal/pallas_call | solution.py:706

commit v5 on v4

--- a/solution.py
+++ b/solution.py
@@ -16,7 +16,8 @@
 TILE = 640
 FOLD = 512
 ROWS = 10
-WIDTH = 8
+SIDE = 4
+UNROLL = 2
 MODES = 512
 ATOMS = 128
 F32 = jnp.float32
@@ -173,7 +174,7 @@
     w3_all = jnp.concatenate([w3_high, w3_high, w3_low], axis=1)
     sublane = iota((8, ATOMS), 0)
 
-    def group(g, carry):
+    def geometry(g):
         rows = pl.ds(pl.multiple_of(g * 8, 8), 8)
         code = near_ref[rows, :]
         slot = code & 127
@@ -190,37 +191,41 @@
         scaled = [(parts[c] - own_ref[c, rows, :]) * (extent[c] / 24.0) for c in range(3)]
         square = scaled[0] * scaled[0] + scaled[1] * scaled[1] + scaled[2] * scaled[2]
         smooth = 1.0 / (1.0 + square)
-        kind = parts[3]
         scale = smooth * (1.0 / 128.0)
-        radial = [scale] + [scale * scaled[c] for c in range(3)]
-        found = jnp.zeros((32, ATOMS), F32)
-        for pair in range(8 // WIDTH):
-            pieces, blocks = [], []
-            for b in range(WIDTH * pair, WIDTH * pair + WIDTH):
+        return rows, smooth, parts[3], [scale] + [scale * scaled[c] for c in range(3)]
+
+    def group(g, carry):
+        sets = [geometry(g * SIDE + i) for i in range(SIDE)]
+        pieces = []
+        for _, smooth, kind, _ in sets:
+            for b in range(8):
                 s = jnp.broadcast_to(smooth[b : b + 1, :], (32, ATOMS))
                 h = jnp.broadcast_to(kind[b : b + 1, :], (32, ATOMS)) > 0.5
                 pieces.append(
                     jnp.where(h, w_hydrogen, w_oxygen) * s + jnp.where(h, b_hydrogen, b_oxygen)
                 )
-                blocks.append(
-                    jnp.concatenate([jnp.where(sublane == b, r, 0.0) for r in radial], axis=0)
-                )
-            one = jnp.tanh(jnp.concatenate(pieces, axis=1))
-            high, low = split(one)
-            two = jnp.tanh(mm(w2_all, jnp.concatenate([high, low, high], axis=0)))
-            two = two + jnp.concatenate([one, one], axis=0)
-            high, low = split(two)
-            three = jnp.tanh(mm(w3_all, jnp.concatenate([high, low, high], axis=0)))
-            three = three + jnp.concatenate([two, two], axis=0)
-            high, low = split(three)
+        one = jnp.tanh(jnp.concatenate(pieces, axis=1))
+        high, low = split(one)
+        two = jnp.tanh(mm(w2_all, jnp.concatenate([high, low, high], axis=0)))
+        two = two + jnp.concatenate([one, one], axis=0)
+        high, low = split(two)
+        three = jnp.tanh(mm(w3_all, jnp.concatenate([high, low, high], axis=0)))
+        three = three + jnp.concatenate([two, two], axis=0)
+        high, low = split(three)
+        for i, (rows, _, _, radial) in enumerate(sets):
+            blocks = [
+                jnp.concatenate([jnp.where(sublane == b, r, 0.0) for r in radial], axis=0)
+                for b in range(8)
+            ]
             r_high, r_low = split(jnp.concatenate(blocks, axis=1))
-            both = mm(jnp.concatenate([r_high, r_low], axis=0), high, NT)
-            found = found + (both[:32] + both[32:]) + mm(r_high, low, NT)
-        for p in range(4):
-            mat_ref[p, rows, :] = found[p * 8 : (p + 1) * 8]
+            mine = high[:, i * 1024 : (i + 1) * 1024]
+            both = mm(jnp.concatenate([r_high, r_low], axis=0), mine, NT)
+            found = (both[:32] + both[32:]) + mm(r_high, low[:, i * 1024 : (i + 1) * 1024], NT)
+            for p in range(4):
+                mat_ref[p, rows, :] = found[p * 8 : (p + 1) * 8]
         return carry
 
-    lax.fori_loop(0, ATOMS // 8, group, 0, unroll=4)
+    lax.fori_loop(0, ATOMS // 8 // SIDE, group, 0, unroll=UNROLL)
 
     lane = iota((ATOMS, ATOMS), 1)
     entries = None
@@ -420,20 +425,21 @@
     off_y = sites(1, CY) - iota((CY, 256), 0).astype(F32)
     wx, sx = spline(off_x)
     wz, sz = spline(off_z)
-    wave = mm3(
-        (dft_y_ref[0], dft_y_ref[1]),
-        split(jnp.concatenate(spline(off_y), axis=1)),
-    )
-    wave_ref[...] = wave
+    wy, sy = spline(off_y)
+    dft_y = (dft_y_ref[0], dft_y_ref[1])
+    wave = mm3(dft_y, split(wy))
+    wave_ref[:, :256] = wave
+    wave_ref[:, 256:] = sy
     rest = jnp.zeros((TILE - TX * TZ, 256), F32)
-    for at, (left, right) in enumerate(((wz, wx), (wz, sx), (sz, wx))):
+
+    def blend(at, left, right):
         full = jnp.concatenate([left[z : z + 1, :] * right for z in range(TZ)] + [rest], axis=0)
         high, low = split(full)
         mix_ref[0, :, at * 256 : (at + 1) * 256] = high
         mix_ref[1, :, at * 256 : (at + 1) * 256] = low
-    spread = mm3(
-        split(wave[:, :256] * charge), (mix_ref[0, :, :256], mix_ref[1, :, :256]), NT
-    )
+        return high, low
+
+    spread = mm3(split(wave * charge), blend(0, wz, wx), NT)
     for part in range(2):
         for t in range(5):
             out_one[:, part * 5 + t, :] = spread[part * 128 : (part + 1) * 128, t * 128 : (t + 1) * 128]
@@ -470,6 +476,10 @@
 
     exchange(out_one, in_one, 0)
 
+    blend(1, wz, sx)
+    blend(2, sz, wx)
+    wave_ref[:, 256:] = mm3(dft_y, split(wave_ref[:, 256:]))
+
     def build(z, carry):
         cz = fac_z_ref[0, pl.ds(z, 1), :]
         zz = fac_z_ref[1, pl.ds(z, 1), :]
@@ -483,6 +493,15 @@
     cos_e = split(tab_ref[0])
     sin_e = split(tab_ref[1])
 
+    def influence(at, weight):
+        total = green_ref[1] + column_ref[1, at]
+        inverse = jnp.where(total == 0.0, 0.0, 1.0 / jnp.where(total == 0.0, 1.0, total))
+        return green_ref[0] * (inverse * (column_ref[0, at] * weight))
+
+    first = me == 0
+    weight = jnp.where(first, 1.0, 2.0)
+    green_a = influence(me, weight)
+    green_b = influence(jnp.where(first, 128, me), weight)
     settle(out_one, in_one, 0)
 
     def gathered(in_ref):
@@ -510,15 +529,6 @@
     real = by_cos[:128] + by_sin[128:]
     imag = by_cos[128:] - by_sin[:128]
 
-    def influence(at, weight):
-        total = green_ref[1] + column_ref[1, at]
-        inverse = jnp.where(total == 0.0, 0.0, 1.0 / jnp.where(total == 0.0, 1.0, total))
-        return green_ref[0] * (inverse * (column_ref[0, at] * weight))
-
-    first = me == 0
-    weight = jnp.where(first, 1.0, 2.0)
-    green_a = influence(me, weight)
-    green_b = influence(jnp.where(first, 128, me), weight)
     modes = split(
         jnp.concatenate(
             [green_a * real, green_a * imag, green_b * real, green_b * imag], axis=0

time: 64.9 us -> 63.4 us (0.977)
  Pallas kernels: 64 us -> 62.6 us
    pallas_call x1, Pallas kernels: 49.6 us -> 48.1 us  [local(): pl.pallas_call(main_kernel, out_shape=jax.ShapeDtypeStruct((24, ATOMS), F...]
where the time goes in v5:
time: 63.4 us; the launch traced here: 63.2 us
  Pallas kernels  62.6 us (99%)
  between operations  0.65 us (1%)
    pallas_call x1, Pallas kernels, local(): pl.pallas_call(main_kernel, out_shape=jax.ShapeDtypeStruct((24, ATOMS), F...  48.1 us
    pallas_call x1, Pallas kernels, halo(): pl.pallas_call(halo_kernel, out_shape=jax.ShapeDtypeStruct((9, 8, ATOMS),...  13.2 us
    pallas_call x1, Pallas kernels, local(): pl.pallas_call(deal_kernel, out_shape=(jax.ShapeDtypeStruct((3, 1, 1, 1,...  1.3 us

profile of v5, /device:TPU:1, one launch (start us, length us, event | category | flops | bytes accessed | tf_op | source)
XLA Modules:
  0.0 63.2 jit_solution(16594082802699949429)
XLA Ops:
  0.6 13.2 %halo.1.refs_1_ = f32[9,8,128]{2,1,0:T(8,128)} custom-call(f32[3,1,1,1,128]{4,3,2,1,0:T(1,128)} %positions_ref.1, s32[1,1,1,128]{3,2,1,0:T(1,128)} %species_ref.1), custom_call_target="tpu_custom_call" | custom-call | tf_op jit(solution)/shard_map/halo/pallas_call | solution.py:99
  13.8 48.1 %main.1.result_ref = f32[24,128]{1,0:T(8,128)} custom-call(f32[2,129]{1,0:T(2,128)} %constant.20.clone.refs_0_, f32[9,8,128]{2,1,0:T(8,128)} %halo.1.refs_1_, s32[128,128]{1,0:T(8,128)} %bitcast.11, f32[2,25]{1,0:T(2,128)} %refs_3_.1, f32[2,25]{1,0:T(2,128)} %refs_4_.1, f32[25,50]{1,0:T(8,128)} %refs_5_.1, f32[1,50]{1,0:T(1,128)} %bitcast.15, ...), custom_call_target="tpu_custom_call" | custom-call | tf_op jit(solution)/shard_map/main/pallas_call | solution.py:672
  61.9 1.3 %deal.1 = (f32[3,1,1,1,128]{4,3,2,1,0:T(1,128)}, f32[4,1,1,1,128]{4,3,2,1,0:T(1,128)}, f32[4,1,1,1,128]{4,3,2,1,0:T(1,128)}, f32[1,1]{1,0:T(1,128)}) custom-call(f32[24,128]{1,0:T(8,128)} %main.1.result_ref), custom_call_target="tpu_custom_call" | custom-call | tf_op jit(solution)/shard_map/deal/pallas_call | solution.py:716

commit v6 on v5

--- a/solution.py
+++ b/solution.py
@@ -354,6 +354,8 @@
         mix_ref,
         wave_ref,
         tab_ref,
+        plane_ref,
+        field_ref,
         out_one,
         in_one,
         out_two,
@@ -485,13 +487,17 @@
         zz = fac_z_ref[1, pl.ds(z, 1), :]
         cx, xx = fac_x_ref[0], fac_x_ref[1]
         rows = pl.ds(pl.multiple_of(z * TX, 8), TX)
-        tab_ref[0, rows, :] = cx * cz - xx * zz
-        tab_ref[1, rows, :] = xx * cz + cx * zz
+        for at, value in enumerate((cx * cz - xx * zz, xx * cz + cx * zz)):
+            high, low = split(value)
+            tab_ref[at, 0, rows, :] = high
+            tab_ref[at, 1, rows, :] = low
         return carry
 
     lax.fori_loop(0, 16, build, 0)
-    cos_e = split(tab_ref[0])
-    sin_e = split(tab_ref[1])
+
+    def tile_tables():
+        return [(tab_ref[at, 0], tab_ref[at, 1]) for at in range(2)]
+
 
     def influence(at, weight):
         total = green_ref[1] + column_ref[1, at]
@@ -500,8 +506,8 @@
 
     first = me == 0
     weight = jnp.where(first, 1.0, 2.0)
-    green_a = influence(me, weight)
-    green_b = influence(jnp.where(first, 128, me), weight)
+    plane_ref[2] = influence(me, weight)
+    plane_ref[3] = influence(jnp.where(first, 128, me), weight)
     settle(out_one, in_one, 0)
 
     def gathered(in_ref):
@@ -524,37 +530,38 @@
         [turned[:, :128] + turned[:, FOLD:], turned[:, 128:FOLD]], axis=1
     )
     turned = split(turned)
+    cos_e, sin_e = tile_tables()
     by_cos = mm3(turned, cos_e)
     by_sin = mm3(turned, sin_e)
-    real = by_cos[:128] + by_sin[128:]
-    imag = by_cos[128:] - by_sin[:128]
-
-    modes = split(
-        jnp.concatenate(
-            [green_a * real, green_a * imag, green_b * real, green_b * imag], axis=0
-        )
-    )
-    by_cos = mm3(modes, cos_e, NT)
-    by_sin = mm3(modes, sin_e, NT)
-
-    def widen(x):
-        return jnp.concatenate([x, x[:, :128]], axis=1)
-
-    def back(at):
-        real = widen(by_cos[at : at + 128] - by_sin[at + 128 : at + 256])
-        imag = widen(by_sin[at : at + 128] + by_cos[at + 128 : at + 256])
-        return real * cos_t - imag * sin_t, imag * cos_t + real * sin_t
-
-    real_a, imag_a = back(0)
-    real_b, imag_b = back(256)
-    field_r = mm3(
-        (dft_b_ref[0, :128], dft_b_ref[1, :128]),
-        split(jnp.concatenate([real_a, -imag_a], axis=0)),
-    )
-    field_i = mm3(
-        (dft_b_ref[0, 128:], dft_b_ref[1, 128:]),
-        split(jnp.concatenate([-real_b, imag_b], axis=0)),
-    )
+    plane_ref[0] = by_cos[:128] + by_sin[128:]
+    plane_ref[1] = by_cos[128:] - by_sin[:128]
+
+    def inverse(at):
+        cos_e, sin_e = tile_tables()
+        green = plane_ref[at]
+        modes = split(jnp.concatenate([green * plane_ref[0], green * plane_ref[1]], axis=0))
+        by_cos = mm3(modes, cos_e, NT)
+        by_sin = mm3(modes, sin_e, NT)
+        real = by_cos[:128] - by_sin[128:]
+        imag = by_sin[:128] + by_cos[128:]
+        real = jnp.concatenate([real, real[:, :128]], axis=1)
+        imag = jnp.concatenate([imag, imag[:, :128]], axis=1)
+        cos_t, sin_t = twiddle_ref[0], twiddle_ref[1]
+        real, imag = real * cos_t - imag * sin_t, imag * cos_t + real * sin_t
+        return split(jnp.concatenate([real, -imag], axis=0))
+
+    @pl.when(me != 0)
+    def _():
+        both = mm3((dft_b_ref[0], dft_b_ref[1]), inverse(2))
+        field_ref[0] = both[:128]
+        field_ref[1] = -both[128:]
+
+    @pl.when(me == 0)
+    def _():
+        field_ref[0] = mm3((dft_b_ref[0, :128], dft_b_ref[1, :128]), inverse(2))
+        field_ref[1] = -mm3((dft_b_ref[0, 128:], dft_b_ref[1, 128:]), inverse(3))
+
+    field_r, field_i = field_ref[0], field_ref[1]
     partial = jnp.sum(tiles[:128] * field_r + tiles[128:] * field_i, keepdims=True)
     partial = partial * (0.5 / (ND * ATOMS))
     lane = iota((ND, 128), 1)
@@ -681,7 +688,9 @@
             pltpu.VMEM((4, ATOMS, ATOMS), F32),
             pltpu.VMEM((2, TILE, 768), BF16),
             pltpu.VMEM((CY, 512), F32),
-            pltpu.VMEM((2, FOLD, MODES), F32),
+            pltpu.VMEM((2, 2, FOLD, MODES), BF16),
+            pltpu.VMEM((4, ND, MODES), F32),
+            pltpu.VMEM((2, ND, TILE), F32),
             pltpu.VMEM((ND, ROWS, 128), F32),
             pltpu.VMEM((ND, ROWS, 128), F32),
             pltpu.VMEM((ND, ROWS, 128), F32),

time: 63.4 us -> 61.3 us (0.967)
  Pallas kernels: 62.6 us -> 60.4 us
    pallas_call x1, Pallas kernels: 48.1 us -> 46 us  [local(): pl.pallas_call(main_kernel, out_shape=jax.ShapeDtypeStruct((24, ATOMS), F...]
where the time goes in v6:
time: 61.3 us; the launch traced here: 61.1 us
  Pallas kernels  60.4 us (99%)
  between operations  0.65 us (1%)
    pallas_call x1, Pallas kernels, local(): pl.pallas_call(main_kernel, out_shape=jax.ShapeDtypeStruct((24, ATOMS), F...  46 us
    pallas_call x1, Pallas kernels, halo(): pl.pallas_call(halo_kernel, out_shape=jax.ShapeDtypeStruct((9, 8, ATOMS),...  13.2 us
    pallas_call x1, Pallas kernels, local(): pl.pallas_call(deal_kernel, out_shape=(jax.ShapeDtypeStruct((3, 1, 1, 1,...  1.3 us

profile of v6, /device:TPU:1, one launch (start us, length us, event | category | flops | bytes accessed | tf_op | source)
XLA Modules:
  0.0 61.1 jit_solution(12233362267422813046)
XLA Ops:
  0.6 13.2 %halo.1.refs_1_ = f32[9,8,128]{2,1,0:T(8,128)} custom-call(f32[3,1,1,1,128]{4,3,2,1,0:T(1,128)} %positions_ref.1, s32[1,1,1,128]{3,2,1,0:T(1,128)} %species_ref.1), custom_call_target="tpu_custom_call" | custom-call | tf_op jit(solution)/shard_map/halo/pallas_call | solution.py:99
  13.8 46.0 %main.1.result_ref = f32[24,128]{1,0:T(8,128)} custom-call(f32[2,129]{1,0:T(2,128)} %constant.20.clone.refs_0_, f32[9,8,128]{2,1,0:T(8,128)} %halo.1.refs_1_, s32[128,128]{1,0:T(8,128)} %bitcast.11, f32[2,25]{1,0:T(2,128)} %refs_3_.1, f32[2,25]{1,0:T(2,128)} %refs_4_.1, f32[25,50]{1,0:T(8,128)} %refs_5_.1, f32[1,50]{1,0:T(1,128)} %bitcast.15, ...), custom_call_target="tpu_custom_call" | custom-call | tf_op jit(solution)/shard_map/main/pallas_call | solution.py:679
  59.8 1.3 %deal.1 = (f32[3,1,1,1,128]{4,3,2,1,0:T(1,128)}, f32[4,1,1,1,128]{4,3,2,1,0:T(1,128)}, f32[4,1,1,1,128]{4,3,2,1,0:T(1,128)}, f32[1,1]{1,0:T(1,128)}) custom-call(f32[24,128]{1,0:T(8,128)} %main.1.result_ref), custom_call_target="tpu_custom_call" | custom-call | tf_op jit(solution)/shard_map/deal/pallas_call | solution.py:725

commit v7 on v6

--- a/solution.py
+++ b/solution.py
@@ -374,15 +374,27 @@
     me = wide * NN + narrow
     barrier = pltpu.get_barrier_semaphore()
 
-    def peer(d):
-        at = lax.rem(me + d, ND)
-        return at, (at // NN, lax.rem(at, NN))
-
-    def greet(d, carry):
-        pl.semaphore_signal(barrier, inc=1, device_id=peer(d)[1], device_id_type=MESH)
-        return carry
-
-    lax.fori_loop(1, ND, greet, 0)
+    def everyone(act):
+        def close(i, carry):
+            act(0, i + 1)
+            return carry
+
+        def distant(i, carry):
+            act(1 + i // NN, lax.rem(i, NN))
+            return carry
+
+        lax.fori_loop(0, NN - 1, close, 0, unroll=5)
+        lax.fori_loop(0, (NW - 1) * NN, distant, 0, unroll=8)
+
+    def device(step_w, step_n):
+        return lax.rem(wide + step_w, NW), lax.rem(narrow + step_n, NN)
+
+    def greet(step_w, step_n):
+        pl.semaphore_signal(
+            barrier, inc=1, device_id=device(step_w, step_n), device_id_type=MESH
+        )
+
+    everyone(greet)
 
     def arrived():
         for copy in fetch[len(EARLY) :]:
@@ -448,20 +460,19 @@
 
     pl.semaphore_wait(barrier, ND - 1)
 
-    def exchange(out_ref, in_ref, s):
-        def one(d, carry):
-            at, device = peer(d)
+    def exchange(out_ref, in_ref, s, slot):
+        def one(step_w, step_n):
+            w, n = device(step_w, step_n)
             pltpu.make_async_remote_copy(
-                src_ref=out_ref.at[at],
+                src_ref=out_ref.at[w * NN + n],
                 dst_ref=in_ref.at[me],
                 send_sem=send_sem.at[s],
-                recv_sem=recv_sem.at[s],
-                device_id=device,
+                recv_sem=recv_sem.at[slot(step_w)],
+                device_id=(w, n),
                 device_id_type=MESH,
             ).start()
-            return carry
-
-        lax.fori_loop(1, ND, one, 0)
+
+        everyone(one)
         in_ref[me] = out_ref[me]
 
     def settle(out_ref, in_ref, s):
@@ -470,13 +481,13 @@
             dst_ref=in_ref.at[pl.ds(0, ND - 1)],
             send_sem=send_sem.at[s],
             recv_sem=recv_sem.at[s],
-            device_id=peer(1)[1],
+            device_id=device(0, 1),
             device_id_type=MESH,
         )
         whole.wait_send()
         whole.wait_recv()
 
-    exchange(out_one, in_one, 0)
+    exchange(out_one, in_one, 0, lambda step_w: 0)
 
     blend(1, wz, sx)
     blend(2, sz, wx)
@@ -572,28 +583,7 @@
         out_two[:, t, :] = piece
         out_two[:, 5 + t, :] = field_i[:, t * 128 : (t + 1) * 128]
 
-    def place(c, i):
-        step = c * 2 + i // NN
-        w = lax.rem(wide + step, NW)
-        n = lax.rem(narrow + lax.rem(i, NN), NN)
-        return w * NN + n, (w, n)
-
-    for c in range(4):
-
-        def one(i, carry):
-            at, device = place(c, i)
-            pltpu.make_async_remote_copy(
-                src_ref=out_two.at[at],
-                dst_ref=in_two.at[me],
-                send_sem=send_sem.at[1],
-                recv_sem=recv_sem.at[1 + c],
-                device_id=device,
-                device_id_type=MESH,
-            ).start()
-            return carry
-
-        lax.fori_loop(1 if c == 0 else 0, 32, one, 0)
-    in_two[me] = out_two[me]
+    exchange(out_two, in_two, 1, lambda step_w: 1 + step_w // 2)
     mix = (mix_ref[0], mix_ref[1])
     rows = [jnp.zeros((1, 256), F32)] * 4
     total = jnp.zeros((1, 1), F32)
@@ -604,7 +594,7 @@
             dst_ref=in_two.at[pl.ds(0, size)],
             send_sem=send_sem.at[1],
             recv_sem=recv_sem.at[1 + c],
-            device_id=peer(1)[1],
+            device_id=device(0, 1),
             device_id_type=MESH,
         ).wait_recv()
         spans = [lax.rem(wide + (NW - 2 * c - i), NW) * NN for i in range(2)]
@@ -634,7 +624,7 @@
         dst_ref=in_two.at[pl.ds(0, ND - 1)],
         send_sem=send_sem.at[1],
         recv_sem=recv_sem.at[1],
-        device_id=peer(1)[1],
+        device_id=device(0, 1),
         device_id_type=MESH,
     ).wait_send()
     atom = [r[:, :128] for r in rows]

time: 61.3 us -> 60.5 us (0.987)
  Pallas kernels: 60.4 us -> 59.6 us
    pallas_call x1, Pallas kernels: 46 us -> 45.1 us  [local(): pl.pallas_call(main_kernel, out_shape=jax.ShapeDtypeStruct((24, ATOMS), F...]
where the time goes in v7:
time: 60.5 us; the launch traced here: 60.2 us
  Pallas kernels  59.6 us (99%)
  between operations  0.65 us (1%)
    pallas_call x1, Pallas kernels, local(): pl.pallas_call(main_kernel, out_shape=jax.ShapeDtypeStruct((24, ATOMS), F...  45.1 us
    pallas_call x1, Pallas kernels, halo(): pl.pallas_call(halo_kernel, out_shape=jax.ShapeDtypeStruct((9, 8, ATOMS),...  13.2 us
    pallas_call x1, Pallas kernels, local(): pl.pallas_call(deal_kernel, out_shape=(jax.ShapeDtypeStruct((3, 1, 1, 1,...  1.3 us

profile of v7, /device:TPU:1, one launch (start us, length us, event | category | flops | bytes accessed | tf_op | source)
XLA Modules:
  0.0 60.2 jit_solution(9075654682629059923)
XLA Ops:
  0.6 13.2 %halo.1.refs_1_ = f32[9,8,128]{2,1,0:T(8,128)} custom-call(f32[3,1,1,1,128]{4,3,2,1,0:T(1,128)} %positions_ref.1, s32[1,1,1,128]{3,2,1,0:T(1,128)} %species_ref.1), custom_call_target="tpu_custom_call" | custom-call | tf_op jit(solution)/shard_map/halo/pallas_call | solution.py:99
  13.8 45.1 %main.1.result_ref = f32[24,128]{1,0:T(8,128)} custom-call(f32[2,129]{1,0:T(2,128)} %constant.20.clone.refs_0_, f32[9,8,128]{2,1,0:T(8,128)} %halo.1.refs_1_, s32[128,128]{1,0:T(8,128)} %bitcast.11, f32[2,25]{1,0:T(2,128)} %refs_3_.1, f32[2,25]{1,0:T(2,128)} %refs_4_.1, f32[25,50]{1,0:T(8,128)} %refs_5_.1, f32[1,50]{1,0:T(1,128)} %bitcast.15, ...), custom_call_target="tpu_custom_call" | custom-call | tf_op jit(solution)/shard_map/main/pallas_call | solution.py:669
  58.9 1.3 %deal.1 = (f32[3,1,1,1,128]{4,3,2,1,0:T(1,128)}, f32[4,1,1,1,128]{4,3,2,1,0:T(1,128)}, f32[4,1,1,1,128]{4,3,2,1,0:T(1,128)}, f32[1,1]{1,0:T(1,128)}) custom-call(f32[24,128]{1,0:T(8,128)} %main.1.result_ref), custom_call_target="tpu_custom_call" | custom-call | tf_op jit(solution)/shard_map/deal/pallas_call | solution.py:715

commit v8 on v7

--- a/solution.py
+++ b/solution.py
@@ -16,8 +16,8 @@
 TILE = 640
 FOLD = 512
 ROWS = 10
-SIDE = 4
-UNROLL = 2
+SIDE = 8
+UNROLL = 1
 MODES = 512
 ATOMS = 128
 F32 = jnp.float32

time: 60.5 us -> 61.1 us (level)
    pallas_call x1, Pallas kernels: 45.1 us -> 45.8 us  [local(): pl.pallas_call(main_kernel, out_shape=jax.ShapeDtypeStruct((24, ATOMS), F...]
where the time goes in v8:
time: 61.1 us; the launch traced here: 60.9 us
  Pallas kernels  60.2 us (99%)
  between operations  0.65 us (1%)
    pallas_call x1, Pallas kernels, local(): pl.pallas_call(main_kernel, out_shape=jax.ShapeDtypeStruct((24, ATOMS), F...  45.8 us
    pallas_call x1, Pallas kernels, halo(): pl.pallas_call(halo_kernel, out_shape=jax.ShapeDtypeStruct((9, 8, ATOMS),...  13.2 us
    pallas_call x1, Pallas kernels, local(): pl.pallas_call(deal_kernel, out_shape=(jax.ShapeDtypeStruct((3, 1, 1, 1,...  1.3 us

profile of v8, /device:TPU:1, one launch (start us, length us, event | category | flops | bytes accessed | tf_op | source)
XLA Modules:
  0.0 60.9 jit_solution(16051219372704870062)
XLA Ops:
  0.6 13.2 %halo.1.refs_1_ = f32[9,8,128]{2,1,0:T(8,128)} custom-call(f32[3,1,1,1,128]{4,3,2,1,0:T(1,128)} %positions_ref.1, s32[1,1,1,128]{3,2,1,0:T(1,128)} %species_ref.1), custom_call_target="tpu_custom_call" | custom-call | tf_op jit(solution)/shard_map/halo/pallas_call | solution.py:99
  13.8 45.8 %main.1.result_ref = f32[24,128]{1,0:T(8,128)} custom-call(f32[2,129]{1,0:T(2,128)} %constant.20.clone.refs_0_, f32[9,8,128]{2,1,0:T(8,128)} %halo.1.refs_1_, s32[128,128]{1,0:T(8,128)} %bitcast.11, f32[2,25]{1,0:T(2,128)} %refs_3_.1, f32[2,25]{1,0:T(2,128)} %refs_4_.1, f32[25,50]{1,0:T(8,128)} %refs_5_.1, f32[1,50]{1,0:T(1,128)} %bitcast.15, ...), custom_call_target="tpu_custom_call" | custom-call | tf_op jit(solution)/shard_map/main/pallas_call | solution.py:669
  59.6 1.3 %deal.1 = (f32[3,1,1,1,128]{4,3,2,1,0:T(1,128)}, f32[4,1,1,1,128]{4,3,2,1,0:T(1,128)}, f32[4,1,1,1,128]{4,3,2,1,0:T(1,128)}, f32[1,1]{1,0:T(1,128)}) custom-call(f32[24,128]{1,0:T(8,128)} %main.1.result_ref), custom_call_target="tpu_custom_call" | custom-call | tf_op jit(solution)/shard_map/deal/pallas_call | solution.py:715
